TPU v7x, 32 devices: a whole 2x2x4 slice. The times are simulated.
32 devices in a mesh: grp: 4 (over y, core), tp: 8 (over z, x).
Axes of the slice: x: 2, y: 2, z: 4, core: 2. Of those that a mesh axis runs over, the one named last changes fastest.
Arguments:
- tokens: bfloat16 [64, 256, 1152], P(('grp', 'tp')), may hold values from -4 to 4
- cond: bfloat16 [64, 1152], P('grp'), may hold values from -2 to 2
- keep_counts: int32 [64], P('grp'), may hold values from 64 to 192, as said below
- orders: int32 [64, 256], P('grp'), may hold values from 0 to 255, each once within a row
- ada_weight: bfloat16 [1152, 6, 1152], P(None, None, 'tp'), may hold values from -0.1875 to 0.1875
- ada_bias: bfloat16 [6, 1152], P(None, 'tp'), may hold values from -0.3984375 to 0.3984375
- qkv_weight: bfloat16 [1152, 3, 1152], P(None, None, 'tp'), may hold values from -0.1875 to 0.1875
- qv_bias: bfloat16 [2, 1152], P(None, 'tp'), may hold values from -0.3984375 to 0.3984375
- out_weight: bfloat16 [1152, 1152], P('tp'), may hold values from -0.75 to 0.75
- out_bias: bfloat16 [1152], replicated, may hold values from -0.3984375 to 0.3984375
- fc1_weight: bfloat16 [1152, 4608], P(None, 'tp'), may hold values from -0.1875 to 0.1875
- fc1_bias: bfloat16 [4608], P('tp'), may hold values from -0.3984375 to 0.3984375
- fc2_weight: bfloat16 [4608, 1152], P('tp'), may hold values from -0.09375 to 0.09375
- fc2_bias: bfloat16 [1152], replicated, may hold values from -0.3984375 to 0.3984375
- cotangent: bfloat16 [64, 256, 1152], P(('grp', 'tp')), may hold values from -4 to 4
Outputs:
- block_out: float32 [64, 256, 1152], P(('grp', 'tp'))
- tokens_grad: float32 [64, 256, 1152], P(('grp', 'tp'))
- cond_grad: float32 [64, 1152], P('grp', 'tp')
- ada_weight_grad: float32 [1152, 6, 1152], P(None, None, 'tp')
- ada_bias_grad: float32 [6, 1152], P(None, 'tp')
- qkv_weight_grad: float32 [1152, 3, 1152], P(None, None, 'tp')
- qv_bias_grad: float32 [2, 1152], P(None, 'tp')
- out_weight_grad: float32 [1152, 1152], P('tp')
- out_bias_grad: float32 [1152], P('tp')
- fc1_weight_grad: float32 [1152, 4608], P(None, 'tp')
- fc1_bias_grad: float32 [4608], P('tp')
- fc2_weight_grad: float32 [4608, 1152], P('tp')
- fc2_bias_grad: float32 [1152], P('tp')
- token_counts: int32 [2], replicated
Inputs may be any that keep to these rules, and one draw needn't show every extreme that they name: `keep_counts`: the images of a group keep counts near a common level, which rises from the first group to the last. `orders`: each row holds every number of 0 to 255 once.
All inputs are finite; a program needn't handle non-finite values.
Results may differ from a plain program's by a relative error of at most 0.02.
Values may be sent and summed in bfloat16 or wider, within the bound.
A program may use at most 320 MiB of HBM per device.

v0:
```python
import jax
import jax.numpy as jnp
from jax import lax
from jax.sharding import PartitionSpec as P

HEAD_DIM = 72


WIDE_TYPE = jnp.float32
HALF_TYPE = jnp.bfloat16


def layer_stats(values):
    centred = values - jnp.mean(values, axis=-1, keepdims=True)
    inv_std = lax.rsqrt(jnp.mean(centred * centred, axis=-1, keepdims=True) + 1e-06)
    return (centred * inv_std, inv_std)


def layer_back(grad_norm, normed, inv_std):
    mean_grad = jnp.mean(grad_norm, axis=-1, keepdims=True)
    mean_proj = jnp.mean(grad_norm * normed, axis=-1, keepdims=True)
    return inv_std * (grad_norm - mean_grad - normed * mean_proj)


def kept_mask(counts_in, orders_in):
    tok_count = orders_in.shape[1]
    places = lax.broadcasted_iota(jnp.int32, (1, 1, tok_count), 2)
    slot_ids = lax.broadcasted_iota(jnp.int32, (1, tok_count, 1), 1)
    position = jnp.sum(jnp.where(orders_in[:, :, None] == places, slot_ids, 0), axis=1)
    return (position < counts_in[:, None]).astype(WIDE_TYPE)


def gelu_tanh(values):
    return jax.nn.gelu(values, approximate=True)


def masked_scores(qkv_parts, key_mask):
    scores = jnp.einsum(
        "iqhe,ikhe->ihqk", qkv_parts[:, :, 0], qkv_parts[:, :, 1], preferred_element_type=WIDE_TYPE
    ) * HEAD_DIM ** (-0.5)
    return jnp.where(key_mask[:, None, None, :] > 0.5, scores, -1e30)


def attend(attn_rows, qkv_use, qv_use, key_mask):
    images, tok_count = key_mask.shape
    local_width = qkv_use.shape[2]
    head_count = local_width // HEAD_DIM
    projected = jnp.einsum("rd,dke->rke", attn_rows, qkv_use, preferred_element_type=WIDE_TYPE)
    bias_wide = qv_use.astype(WIDE_TYPE)
    bias_all = jnp.stack([bias_wide[0], jnp.zeros_like(bias_wide[0]), bias_wide[1]])
    projected = (projected + bias_all[None]).astype(HALF_TYPE)
    qkv_parts = projected.reshape(images, tok_count, 3, head_count, HEAD_DIM)
    scores = masked_scores(qkv_parts, key_mask)
    row_max = jnp.max(scores, axis=-1, keepdims=True)
    exps_raw = jnp.exp(scores - row_max)
    row_total = jnp.sum(exps_raw, axis=-1, keepdims=True)
    attn_probs = (exps_raw / row_total).astype(HALF_TYPE)
    log_total = row_max + jnp.log(row_total)
    attn_out = jnp.einsum(
        "ihqk,ikhe->iqhe", attn_probs, qkv_parts[:, :, 2], preferred_element_type=WIDE_TYPE
    )
    attn_out = attn_out.astype(HALF_TYPE).reshape(images * tok_count, local_width)
    return (projected, log_total, attn_out)


def attend_back(projected, log_total, grad_attn, key_mask):
    images, tok_count = key_mask.shape
    local_width = projected.shape[2]
    head_count = local_width // HEAD_DIM
    qkv_parts = projected.reshape(images, tok_count, 3, head_count, HEAD_DIM)
    attn_probs = jnp.exp(masked_scores(qkv_parts, key_mask) - log_total)
    grad_heads = grad_attn.reshape(images, tok_count, head_count, HEAD_DIM)
    grad_values = jnp.einsum(
        "ihqk,iqhe->ikhe",
        attn_probs.astype(HALF_TYPE),
        grad_heads,
        preferred_element_type=WIDE_TYPE,
    )
    grad_probs = jnp.einsum(
        "iqhe,ikhe->ihqk", grad_heads, qkv_parts[:, :, 2], preferred_element_type=WIDE_TYPE
    )
    grad_scores = attn_probs * (
        grad_probs - jnp.sum(attn_probs * grad_probs, axis=-1, keepdims=True)
    )
    grad_scores = grad_scores.astype(HALF_TYPE)
    scale_factor = HEAD_DIM ** (-0.5)
    grad_queries = (
        jnp.einsum(
            "ihqk,ikhe->iqhe", grad_scores, qkv_parts[:, :, 1], preferred_element_type=WIDE_TYPE
        )
        * scale_factor
    )
    grad_keys = (
        jnp.einsum(
            "ihqk,iqhe->ikhe", grad_scores, qkv_parts[:, :, 0], preferred_element_type=WIDE_TYPE
        )
        * scale_factor
    )
    grad_all = jnp.stack([grad_queries, grad_keys, grad_values], axis=2)
    return grad_all.reshape(images * tok_count, 3, local_width).astype(HALF_TYPE)


def body(
    tokens,
    cond,
    keep_counts,
    orders,
    ada_weight,
    ada_bias,
    qkv_weight,
    qv_bias,
    out_weight,
    out_bias,
    fc1_weight,
    fc1_bias,
    fc2_weight,
    fc2_bias,
    cotangent,
):
    tp_rank = lax.axis_index("tp")
    tp_count = lax.axis_size("tp")
    img_dev, tok_count, model_width = tokens.shape
    img_group = cond.shape[0]
    row_count = img_dev * tok_count
    part_width = model_width // tp_count
    mask_group = kept_mask(keep_counts, orders)
    mask_own = lax.dynamic_slice_in_dim(mask_group, tp_rank * img_dev, img_dev, 0)
    keep_col = mask_own[:, :, None]
    silu_cond = jax.nn.silu(cond.astype(WIDE_TYPE)).astype(HALF_TYPE)
    ada_cols = (
        jnp.einsum("id,dke->ike", silu_cond, ada_weight, preferred_element_type=WIDE_TYPE)
        + ada_bias.astype(WIDE_TYPE)[None]
    )
    modulation = lax.all_to_all(ada_cols, "tp", split_axis=0, concat_axis=2, tiled=True)
    shift_one = modulation[:, 0][:, None, :]
    scale_one = modulation[:, 1][:, None, :]
    gate_one = modulation[:, 2][:, None, :]
    shift_two = modulation[:, 3][:, None, :]
    scale_two = modulation[:, 4][:, None, :]
    gate_two = modulation[:, 5][:, None, :]
    resid_rows = tokens.astype(WIDE_TYPE)
    normed_one, inv_one = layer_stats(resid_rows)
    attn_in = (
        (normed_one * (1.0 + scale_one) + shift_one)
        .astype(HALF_TYPE)
        .reshape(row_count, model_width)
    )
    qkv_use, qv_use, out_use, fc1_use, fc1b_use, fc2_use = (
        qkv_weight,
        qv_bias,
        out_weight,
        fc1_weight,
        fc1_bias,
        fc2_weight,
    )
    attn_rows = lax.all_gather(attn_in, "tp", axis=0, tiled=True)
    projected, log_total, attn_out = attend(attn_rows, qkv_use, qv_use, mask_group)
    branch_one = lax.psum_scatter(
        jnp.dot(attn_out, out_use, preferred_element_type=WIDE_TYPE),
        "tp",
        scatter_dimension=0,
        tiled=True,
    )
    branch_one = (branch_one + out_bias.astype(WIDE_TYPE)).reshape(img_dev, tok_count, model_width)
    hidden_res = resid_rows + keep_col * gate_one * branch_one
    normed_two, inv_two = layer_stats(hidden_res)
    mlp_in = (
        (normed_two * (1.0 + scale_two) + shift_two)
        .astype(HALF_TYPE)
        .reshape(row_count, model_width)
    )
    mlp_rows = lax.all_gather(mlp_in, "tp", axis=0, tiled=True)
    pre_act = jnp.dot(mlp_rows, fc1_use, preferred_element_type=WIDE_TYPE) + fc1b_use.astype(
        WIDE_TYPE
    )
    activated = gelu_tanh(pre_act).astype(HALF_TYPE)
    branch_two = lax.psum_scatter(
        jnp.dot(activated, fc2_use, preferred_element_type=WIDE_TYPE).astype(jnp.bfloat16),
        "tp",
        scatter_dimension=0,
        tiled=True,
    ).astype(jnp.float32)
    branch_two = (branch_two + fc2_bias.astype(WIDE_TYPE)).reshape(img_dev, tok_count, model_width)
    block_out = hidden_res + keep_col * gate_two * branch_two
    grad_out = cotangent.astype(WIDE_TYPE)
    gate_grad_two = jnp.sum(grad_out * keep_col * branch_two, axis=1)
    branch_grad_two = (
        (grad_out * keep_col * gate_two).astype(HALF_TYPE).reshape(row_count, model_width)
    )
    grad_rows_two = lax.all_gather(branch_grad_two, "tp", axis=0, tiled=True)
    fc2_grad = jnp.einsum("rf,rd->fd", activated, grad_rows_two, preferred_element_type=WIDE_TYPE)
    fc2b_grad = jnp.sum(grad_rows_two.astype(WIDE_TYPE), axis=0)
    grad_act = jnp.einsum("rd,fd->rf", grad_rows_two, fc2_use, preferred_element_type=WIDE_TYPE)
    grad_pre = jax.vjp(gelu_tanh, pre_act)[1](grad_act)[0].astype(HALF_TYPE)
    fc1_grad = jnp.einsum("rd,rf->df", mlp_rows, grad_pre, preferred_element_type=WIDE_TYPE)
    fc1b_grad = jnp.sum(grad_pre.astype(WIDE_TYPE), axis=0)
    grad_mlp_in = lax.psum_scatter(
        jnp.einsum("rf,df->rd", grad_pre, fc1_use, preferred_element_type=WIDE_TYPE),
        "tp",
        scatter_dimension=0,
        tiled=True,
    )
    grad_mlp_in = grad_mlp_in.reshape(img_dev, tok_count, model_width)
    shift_grad_two = jnp.sum(grad_mlp_in, axis=1)
    scale_grad_two = jnp.sum(grad_mlp_in * normed_two, axis=1)
    grad_hidden = grad_out + layer_back(grad_mlp_in * (1.0 + scale_two), normed_two, inv_two)
    gate_grad_one = jnp.sum(grad_hidden * keep_col * branch_one, axis=1)
    branch_grad_one = (
        (grad_hidden * keep_col * gate_one).astype(HALF_TYPE).reshape(row_count, model_width)
    )
    grad_rows_one = lax.all_gather(branch_grad_one, "tp", axis=0, tiled=True)
    out_grad = jnp.einsum("re,rd->ed", attn_out, grad_rows_one, preferred_element_type=WIDE_TYPE)
    outb_grad = jnp.sum(grad_rows_one.astype(WIDE_TYPE), axis=0)
    grad_attn = jnp.einsum(
        "rd,ed->re", grad_rows_one, out_use, preferred_element_type=WIDE_TYPE
    ).astype(HALF_TYPE)
    grad_proj = attend_back(projected, log_total, grad_attn, mask_group)
    qkv_grad = jnp.einsum("rd,rke->dke", attn_rows, grad_proj, preferred_element_type=WIDE_TYPE)
    proj_sum = jnp.sum(grad_proj.astype(WIDE_TYPE), axis=0)
    qvb_grad = jnp.stack([proj_sum[0], proj_sum[2]])
    grad_attn_in = lax.psum_scatter(
        jnp.einsum("rke,dke->rd", grad_proj, qkv_use, preferred_element_type=WIDE_TYPE).astype(
            jnp.bfloat16
        ),
        "tp",
        scatter_dimension=0,
        tiled=True,
    ).astype(jnp.float32)
    grad_attn_in = grad_attn_in.reshape(img_dev, tok_count, model_width)
    shift_grad_one = jnp.sum(grad_attn_in, axis=1)
    scale_grad_one = jnp.sum(grad_attn_in * normed_one, axis=1)
    grad_tokens = grad_hidden + layer_back(grad_attn_in * (1.0 + scale_one), normed_one, inv_one)
    modulation_grad = jnp.stack(
        [
            shift_grad_one,
            scale_grad_one,
            gate_grad_one,
            shift_grad_two,
            scale_grad_two,
            gate_grad_two,
        ],
        axis=1,
    ).astype(HALF_TYPE)
    grad_cols = lax.all_to_all(modulation_grad, "tp", split_axis=2, concat_axis=0, tiled=True)
    ada_grad = jnp.einsum("id,ike->dke", silu_cond, grad_cols, preferred_element_type=WIDE_TYPE)
    adab_grad = jnp.sum(grad_cols.astype(WIDE_TYPE), axis=0)
    cond_part = jnp.einsum("ike,dke->id", grad_cols, ada_weight, preferred_element_type=WIDE_TYPE)
    cond_sum = lax.psum_scatter(
        cond_part.astype(jnp.bfloat16), "tp", scatter_dimension=1, tiled=True
    ).astype(jnp.float32)
    cond_cols = lax.dynamic_slice_in_dim(cond, tp_rank * part_width, part_width, 1).astype(
        WIDE_TYPE
    )
    cond_grad = jax.vjp(jax.nn.silu, cond_cols)[1](cond_sum)[0]
    outb_grad = lax.dynamic_slice_in_dim(outb_grad, tp_rank * part_width, part_width, 0)
    fc2b_grad = lax.dynamic_slice_in_dim(fc2b_grad, tp_rank * part_width, part_width, 0)
    group_kept = jnp.sum(keep_counts).astype(WIDE_TYPE)
    summed = (
        lax.psum(ada_grad.astype(jnp.bfloat16), "grp").astype(jnp.float32),
        lax.psum(adab_grad.astype(jnp.bfloat16), "grp").astype(jnp.float32),
        lax.psum(qkv_grad.astype(jnp.bfloat16), "grp").astype(jnp.float32),
        lax.psum(qvb_grad.astype(jnp.bfloat16), "grp").astype(jnp.float32),
        lax.psum(out_grad.astype(jnp.bfloat16), "grp").astype(jnp.float32),
        lax.psum(outb_grad.astype(jnp.bfloat16), "grp").astype(jnp.float32),
        lax.psum(fc1_grad.astype(jnp.bfloat16), "grp").astype(jnp.float32),
        lax.psum(fc1b_grad.astype(jnp.bfloat16), "grp").astype(jnp.float32),
        lax.psum(fc2_grad.astype(jnp.bfloat16), "grp").astype(jnp.float32),
        lax.psum(fc2b_grad.astype(jnp.bfloat16), "grp").astype(jnp.float32),
        lax.psum(group_kept.astype(jnp.bfloat16), "grp").astype(jnp.float32),
    )
    kept_total = summed[10]
    kept_int = kept_total.astype(jnp.int32)
    all_tokens = img_group * tok_count * lax.axis_size("grp")
    token_counts = jnp.stack([kept_int, all_tokens - kept_int])
    return (
        block_out,
        grad_tokens,
        cond_grad,
        summed[0] / kept_total,
        summed[1] / kept_total,
        summed[2] / kept_total,
        summed[3] / kept_total,
        summed[4] / kept_total,
        summed[5] / kept_total,
        summed[6] / kept_total,
        summed[7] / kept_total,
        summed[8] / kept_total,
        summed[9] / kept_total,
        token_counts,
    )


def solution(mesh):
    in_specs = (
        P(("grp", "tp"), None, None),
        P("grp", None),
        P("grp"),
        P("grp", None),
        P(None, None, "tp"),
        P(None, "tp"),
        P(None, None, "tp"),
        P(None, "tp"),
        P("tp", None),
        P(),
        P(None, "tp"),
        P("tp"),
        P("tp", None),
        P(),
        P(("grp", "tp"), None, None),
    )
    out_specs = (
        P(("grp", "tp"), None, None),
        P(("grp", "tp"), None, None),
        P("grp", "tp"),
        P(None, None, "tp"),
        P(None, "tp"),
        P(None, None, "tp"),
        P(None, "tp"),
        P("tp", None),
        P("tp"),
        P(None, "tp"),
        P("tp"),
        P("tp", None),
        P("tp"),
        P(),
    )
    return jax.shard_map(body, mesh=mesh, in_specs=in_specs, out_specs=out_specs, check_vma=False)
```

profile of v0, /device:TPU:0, one launch (start us, length us, event | category | flops | bytes accessed | tf_op | source)
XLA Modules:
  0.0 1863.9 jit_solution(4268364515306655110)
XLA Ops:
  11.0 7.3 all-to-all-start
  19.1 6.0 all-to-all-done
  31.2 133.3 %all-gather.5.cloned.1.call-done = bf16[4096,1152]{1,0:T(8,128)(2,1)} async-done(((bf16[512,1152]{1,0:T(8,128)(2,1)}), bf16[4096,1152]{1,0:T(8,128)(2,1)}) %all-gather.5.cloned.1.call-update) | async-done | bytes 9437200 | tf_op jit(solution)/shard_map/all_gather | solution.py:156
  164.5 7.6 fusion.76
  187.4 8.0 fusion.77
  197.4 306.1 %reduce-scatter.8.cloned.1.call-done = f32[512,1152]{1,0:T(8,128)} async-done(((f32[4096,1152]{1,0:T(8,128)}), f32[512,1152]{1,0:T(8,128)}) %reduce-scatter.8.cloned.1.call-update) | async-done | bytes 2359312 | tf_op jit(solution)/shard_map/reduce_scatter | solution.py:158
  510.2 135.8 %all-gather.7.cloned.1.call-done = bf16[4096,1152]{1,0:T(8,128)(2,1)} async-done(((bf16[512,1152]{1,0:T(8,128)(2,1)}), bf16[4096,1152]{1,0:T(8,128)(2,1)}) %all-gather.7.cloned.1.call-update) | async-done | bytes 9437200 | tf_op jit(solution)/shard_map/all_gather | solution.py:172
  646.0 11.5 fusion.78
  657.5 126.6 %all-gather.9.cloned.1.call-done = bf16[4096,1152]{1,0:T(8,128)(2,1)} async-done(((bf16[512,1152]{1,0:T(8,128)(2,1)}), bf16[4096,1152]{1,0:T(8,128)(2,1)}) %all-gather.9.cloned.1.call-update) | async-done | bytes 9437200 | tf_op jit(solution)/shard_map/all_gather | solution.py:190
  784.1 16.2 fusion.70
  802.4 11.0 fusion.79
  813.9 15.0 convolution_convert_fusion
  830.2 291.2 %reduce-scatter.12.cloned.1.call-done = f32[512,1152]{1,0:T(8,128)} async-done(((f32[4096,1152]{1,0:T(8,128)}), f32[512,1152]{1,0:T(8,128)}) %reduce-scatter.12.cloned.1.call-update) | async-done | bytes 2359312 | tf_op jit(solution)/shard_map/reduce_scatter | solution.py:197
  1124.0 4.6 fusion.34
  1129.2 157.0 %reduce-scatter.10.cloned.1.call-done = bf16[512,1152]{1,0:T(8,128)(2,1)} async-done(((bf16[4096,1152]{1,0:T(8,128)(2,1)}), bf16[512,1152]{1,0:T(8,128)(2,1)}) %reduce-scatter.10.cloned.1.call-update) | async-done | bytes 1179664 | tf_op jit(solution)/shard_map/reduce_scatter | solution.py:177
  1286.2 6.2 fusion.31
  1295.2 136.4 %all-gather.11.cloned.1.call-done = bf16[4096,1152]{1,0:T(8,128)(2,1)} async-done(((bf16[512,1152]{1,0:T(8,128)(2,1)}), bf16[4096,1152]{1,0:T(8,128)(2,1)}) %all-gather.11.cloned.1.call-update) | async-done | bytes 9437200 | tf_op jit(solution)/shard_map/all_gather | solution.py:211
  1431.6 6.9 convolution_convert_fusion.1
  1438.8 5.2 fusion.43
  1444.0 7.0 multiply_reduce_fusion
  1475.7 8.2 bitcast_convert_fusion
  1485.9 5.3 convert_reduce_fusion
  1491.3 11.8 convolution_convert_fusion.3
  1503.1 12.1 convolution_convert_fusion.4
  1515.3 6.0 fusion.80
  1521.4 123.1 %reduce-scatter.14.cloned.1.call-done = bf16[512,1152]{1,0:T(8,128)(2,1)} async-done(((bf16[4096,1152]{1,0:T(8,128)(2,1)}), bf16[512,1152]{1,0:T(8,128)(2,1)}) %reduce-scatter.14.cloned.1.call-update) | async-done | bytes 1179664 | tf_op jit(solution)/shard_map/reduce_scatter | solution.py:221
  1654.7 6.6 convolution_convert_fusion.5
  1669.5 5.0 convert_reduce_fusion.1
  1678.8 4.3 fusion.27
  1683.1 7.5 all-reduce
  1694.2 33.9 %reduce-scatter.16.cloned.1.call-done = bf16[144,16]{1,0:T(8,128)(2,1)} async-done(((bf16[1152,16]{1,0:T(8,128)(2,1)}), bf16[144,16]{1,0:T(8,128)(2,1)}) %reduce-scatter.16.cloned.1.call-update) | async-done | bytes 4624
  1729.6 116.0 %all-reduce.4.cloned.1.call-done = (bf16[1152,6,144]{0,2,1:T(8,128)(2,1)}, bf16[1152,3,144]{0,2,1:T(8,128)(2,1)}, bf16[144,1152]{1,0:T(8,128)(2,1)}, bf16[1152,576]{0,1:T(8,128)(2,1)}, bf16[576,1152]{1,0:T(8,128)(2,1)}) async-done(((bf16[1152,6,144]{0,2,1:T(8,128)(2,1)}, bf16[1152,3,144]{0,2,1:T(8,128)(2,1)}, bf16[144,1152]{1,0:T(8,128)(2,1)}, bf16[1152,576]{0,1:T(8,128)(2,1)}, ...) | async-done | bytes 5971984 | tf_op jit(solution)/shard_map/psum | solution.py:259
  (254 shorter events, 108.4 us)
Async XLA Ops:
  11.0 14.1 all-to-all-start
  18.3 146.1 %all-gather.5.cloned.1.call-start = ((), (), s32[]{:S(2)}) async-start(), calls=%async_computation.7 | async-start | bytes 10616832 | tf_op jit(solution)/shard_map/all_gather | solution.py:156
  19.1 153.0 %copy-start.38 = (f32[2,256]{1,0:T(2,128)}, f32[2,256]{1,0:T(2,128)S(1)}, u32[]{:S(2)}) copy-start(f32[2,256]{1,0:T(2,128)S(1)} %add_rsqrt_fusion.1) | copy-start | bytes 6148
  29.6 473.9 %reduce-scatter.8.cloned.1.call-start = ((), (), s32[]{:S(2)}) async-start(), calls=%async_computation.8 | async-start | bytes 21233664 | tf_op jit(solution)/shard_map/reduce_scatter | solution.py:158
  195.5 450.5 %all-gather.7.cloned.1.call-start = ((), (), s32[]{:S(2)}) async-start(), calls=%async_computation.9 | async-start | bytes 10616832 | tf_op jit(solution)/shard_map/all_gather | solution.py:172
  197.4 308.0 %copy-start.36 = (f32[2,256]{1,0:T(2,128)}, f32[2,256]{1,0:T(2,128)S(1)}, u32[]{:S(2)}) copy-start(f32[2,256]{1,0:T(2,128)S(1)} %constant_dynamic-slice_fusion) | copy-start | bytes 6148
  509.5 274.6 %all-gather.9.cloned.1.call-start = ((), (), s32[]{:S(2)}) async-start(), calls=%async_computation.11 | async-start | bytes 10616832 | tf_op jit(solution)/shard_map/all_gather | solution.py:190
  510.1 611.3 %reduce-scatter.12.cloned.1.call-start = ((), (), s32[]{:S(2)}) async-start(), calls=%async_computation.12 | async-start | bytes 21233664 | tf_op jit(solution)/shard_map/reduce_scatter | solution.py:197
  510.2 303.7 %copy-start.48 = (f32[576]{0:T(1024)}, f32[576]{0:T(1024)S(1)}, u32[]{:S(2)}) copy-start(f32[576]{0:T(1024)S(1)} %convert_element_type.186) | copy-start | bytes 6916
  784.1 18.4 copy-start.55
  813.4 472.7 %reduce-scatter.10.cloned.1.call-start = ((), (), s32[]{:S(2)}) async-start(), calls=%async_computation.10 | async-start | bytes 10616832 | tf_op jit(solution)/shard_map/reduce_scatter | solution.py:177
  829.0 602.6 %all-gather.11.cloned.1.call-start = ((), (), s32[]{:S(2)}) async-start(), calls=%async_computation.13 | async-start | bytes 10616832 | tf_op jit(solution)/shard_map/all_gather | solution.py:211
  1124.0 162.2 %copy-start.14 = (bf16[2,256,1152]{2,1,0:T(8,128)(2,1)S(1)}, bf16[2,256,1152]{2,1,0:T(8,128)(2,1)}, u32[]{:S(2)}) copy-start(bf16[2,256,1152]{2,1,0:T(8,128)(2,1)} %param.29) | copy-start | bytes 3538948
  1295.1 349.3 %reduce-scatter.14.cloned.1.call-start = ((), (), s32[]{:S(2)}) async-start(), calls=%async_computation.14 | async-start | bytes 10616832 | tf_op jit(solution)/shard_map/reduce_scatter | solution.py:221
  1438.8 12.2 slice-start
  1485.9 17.2 slice-start.2
  1491.2 11.8 copy-start.49
  1491.2 24.0 %slice-start.5 = ((s8[9437184]{0:T(1024)(128)(4,1)}), s8[4194304]{0:T(1024)(128)(4,1)S(1)}, s32[]{:S(2)}) async-start(s8[9437184]{0:T(1024)(128)(4,1)} %bitcast.206), calls=%async_computation.22 | async-start | bytes 8388608
  1491.2 24.0 %slice-start.6 = ((s8[9437184]{0:T(1024)(128)(4,1)}), s8[4194304]{0:T(1024)(128)(4,1)S(1)}, s32[]{:S(2)}) async-start(s8[9437184]{0:T(1024)(128)(4,1)} %bitcast.206), calls=%async_computation.23 | async-start | bytes 8388608
  1503.1 12.2 copy-start.12
  1503.1 12.2 slice-start.7
  1515.3 129.1 %copy-start.4 = (bf16[2,256,1152]{2,1,0:T(8,128)(2,1)S(1)}, bf16[2,256,1152]{2,1,0:T(8,128)(2,1)}, u32[]{:S(2)}) copy-start(bf16[2,256,1152]{2,1,0:T(8,128)(2,1)} %param.15) | copy-start | bytes 3538948
  1515.3 129.1 %copy-start.26 = (f32[2,1152]{1,0:T(2,128)S(1)}, f32[2,1152]{1,0:T(2,128)}, u32[]{:S(2)}) copy-start(f32[2,1152]{1,0:T(2,128)} %copy-done.25) | copy-start | bytes 27652
  1515.3 129.1 %copy-start.34 = (f32[2,256]{1,0:T(2,128)S(1)}, f32[2,256]{1,0:T(2,128)}, u32[]{:S(2)}) copy-start(f32[2,256]{1,0:T(2,128)} %copy-done.33) | copy-start | bytes 6148
  1515.3 129.1 %copy-start.39 = (f32[2,256]{1,0:T(2,128)S(1)}, f32[2,256]{1,0:T(2,128)}, u32[]{:S(2)}) copy-start(f32[2,256]{1,0:T(2,128)} %copy-done.38) | copy-start | bytes 6148
  1521.3 126.0 %copy-start.44 = (bf16[2,1152]{1,0:T(2,128)(2,1)S(1)}, bf16[2,1152]{1,0:T(2,128)(2,1)}, u32[]{:S(2)}) copy-start(bf16[2,1152]{1,0:T(2,128)(2,1)} %get-tuple-element.21) | copy-start | bytes 13828
  1521.4 126.0 %copy-start.42 = (bf16[2,1152]{1,0:T(2,128)(2,1)S(1)}, bf16[2,1152]{1,0:T(2,128)(2,1)}, u32[]{:S(2)}) copy-start(bf16[2,1152]{1,0:T(2,128)(2,1)} %get-tuple-element.16) | copy-start | bytes 13828
  1521.4 126.0 %copy-start.41 = (bf16[2,1152]{1,0:T(2,128)(2,1)S(1)}, bf16[2,1152]{1,0:T(2,128)(2,1)}, u32[]{:S(2)}) copy-start(bf16[2,1152]{1,0:T(2,128)(2,1)} %get-tuple-element.14) | copy-start | bytes 13828
  1521.4 126.0 %copy-start.43 = (bf16[2,1152]{1,0:T(2,128)(2,1)S(1)}, bf16[2,1152]{1,0:T(2,128)(2,1)}, u32[]{:S(2)}) copy-start(bf16[2,1152]{1,0:T(2,128)(2,1)} %get-tuple-element.20) | copy-start | bytes 13828
  1651.0 11.4 all-to-all-start.1
  1654.7 73.4 %reduce-scatter.16.cloned.1.call-start = ((), (), s32[]{:S(2)}) async-start(), calls=%async_computation.15 | async-start | bytes 331776
  1667.1 178.5 %all-reduce.4.cloned.1.call-start = ((), (), s32[]{:S(2)}) async-start(), calls=%async_computation.16 | async-start | bytes 11943936 | tf_op jit(solution)/shard_map/psum | solution.py:259
  (46 other events, 188.2 us)
Sparse Core Ops, SparseCore 0:
  29.7 134.7 all-gather.4
  195.6 307.8 reduce-scatter.7
  509.6 136.3 all-gather.6
  648.6 135.4 all-gather.8
  813.6 307.8 reduce-scatter.11
  1124.9 161.2 reduce-scatter.9
  1295.2 136.3 all-gather.10
  1484.1 160.2 reduce-scatter.13
  1667.2 60.8 reduce-scatter.15
  1731.8 113.7 all-reduce.3
where the time goes:
time: 1870 us; the launch traced here: 1860 us
  waiting for transfers between devices  1570 us (84%)
  matrix products  148 us (8%)
  other arithmetic  71.5 us (4%)
  local copies, waits for them, and re-layouts  42 us (2%)
    reduce_scatter x1, waiting for transfers between devices, body(): lax.psum_scatter(jnp.dot(attn_out, out_use, preferred_element_type=WIDE_T...  306 us
    reduce_scatter x1, waiting for transfers between devices, body(): lax.psum_scatter(jnp.einsum('rf,df->rd', grad_pre, fc1_use, preferred_ele...  291 us
    reduce_scatter x1, waiting for transfers between devices, body(): lax.psum_scatter(jnp.dot(activated, fc2_use, preferred_element_type=WIDE_...  157 us
    all_gather x1, waiting for transfers between devices, body(): grad_rows_one = lax.all_gather(branch_grad_one, 'tp', axis=0, tiled=True)  136 us
    all_gather x1, waiting for transfers between devices, body(): mlp_rows = lax.all_gather(mlp_in, 'tp', axis=0, tiled=True)  136 us
    all_gather x1, waiting for transfers between devices, body(): attn_rows = lax.all_gather(attn_in, 'tp', axis=0, tiled=True)  133 us
    all_gather x1, waiting for transfers between devices, body(): grad_rows_two = lax.all_gather(branch_grad_two, 'tp', axis=0, tiled=True)  127 us
    reduce_scatter x1, waiting for transfers between devices, body(): lax.psum_scatter(jnp.einsum('rke,dke->rd', grad_proj, qkv_use, preferred_...  123 us
  transfers between devices with their start and end apart: 12, of which 11 were waited for; matrix products, arithmetic and copies ran while one was open for 5% of the time, Pallas kernels for 0%

commit v1 on v0

v1 whole, which is shorter than its diff:
```python
import functools

import jax
import jax.numpy as jnp
from jax import lax
from jax.experimental import pallas as pl
from jax.experimental.pallas import tpu as pltpu
from jax.sharding import PartitionSpec as P

HEAD_DIM = 72
SCALE = HEAD_DIM ** (-0.5)
F32 = jnp.float32
BF16 = jnp.bfloat16
NT = (((1,), (1,)), ((), ()))
NN = (((1,), (0,)), ((), ()))
TN = (((0,), (0,)), ((), ()))


def dot(a, b, dims):
    return lax.dot_general(a, b, dims, preferred_element_type=F32)


MESH = pl.DeviceIdType.MESH


class Links:
    def __init__(self, tp_count, grp_count):
        self.tp_count = tp_count
        self.cores = 2 if grp_count % 2 == 0 else 1
        self.outer = grp_count // self.cores
        self.steps = (tp_count - 1) // 2
        self.tp = lax.axis_index("tp")
        self.grp = lax.axis_index("grp")
        self.core = self.grp % self.cores
        half = (tp_count + 1) // 2
        self.half = half
        tp = self.tp
        self.place = jnp.where(tp % 2 == 0, tp // 2, half + (tp_count - 1 - tp) // 2)

    def shard(self, distance):
        ring = (self.place + distance + self.tp_count) % self.tp_count
        return jnp.where(ring < self.half, 2 * ring, 2 * (self.tp_count - 1 - ring) + 1)

    def up(self):
        return (self.grp, self.shard(1))

    def down(self):
        return (self.grp, self.shard(-1))

    def sibling(self):
        return (self.grp + 1 - 2 * self.core, self.tp)

    def across(self):
        return ((self.grp + self.cores) % (self.cores * self.outer), self.tp)

    def greet(self, use_core, use_outer, split=True):
        peers = [self.up(), self.down()]
        if use_core:
            peers.append(self.sibling())
        if use_outer and split:
            peers.append(self.across())
        barrier = pltpu.get_barrier_semaphore()
        for peer in peers:
            pl.semaphore_signal(barrier, inc=1, device_id=peer, device_id_type=MESH)
        pl.semaphore_wait(barrier, len(peers))


class Way:
    def __init__(self, tp_count, grp_count, use_core, use_outer, splits):
        self.cores = 2 if use_core else 1
        self.outers = 2 if use_outer else 1
        self.use_core, self.use_outer = use_core, use_outer
        self.shares = self.cores * self.outers
        self.splits = splits
        self.steps = (tp_count - 1) // 2
        self.distances = [0] + [s * d for d in range(1, self.steps + 1) for s in (-1, 1)]
        if tp_count % 2 == 0:
            self.distances.append(tp_count // 2)
        self.arrays = len(splits)

    def share(self, links, outer_flip=0, core_flip=0):
        share = 0
        if self.use_outer:
            share = (links.grp // links.cores + outer_flip) % 2
        if self.use_core:
            share = share * 2 + (links.core + core_flip) % 2
        return share


def remote(src, dst, sems, index, device):
    return pltpu.make_async_remote_copy(
        src_ref=src, dst_ref=dst, send_sem=sems[0].at[index], recv_sem=sems[1].at[index],
        device_id=device, device_id_type=MESH,
    )


def sem_pair(*shape):
    return [pltpu.SemaphoreType.DMA(shape), pltpu.SemaphoreType.DMA(shape)]


class Gather:
    @staticmethod
    def scratch(way):
        n, a = len(way.distances), way.arrays
        shapes = sem_pair(2, a, way.steps + 2)
        shapes += sem_pair(a, n) + sem_pair(2, a, n)
        return shapes + [pltpu.SemaphoreType.DMA((a,))]

    def __init__(self, way, links, own, full, scratch):
        self.way, self.links, self.own, self.full = way, links, own, full
        self.ring, self.outer, self.core = scratch[0:2], scratch[2:4], scratch[4:6]
        self.local = scratch[6]
        self.pending = []

    def slot(self, a, index, **flips):
        way = self.way
        return self.full[a].at[self.links.shard(way.distances[index]), way.share(self.links, **flips)]

    def hop(self, a, index, direction, step, src=None, rows=None):
        src = self.slot(a, index) if src is None else src
        dst = self.slot(a, index)
        if rows is not None:
            src, dst = src.at[rows], dst.at[rows]
        device = self.links.up() if direction == 0 else self.links.down()
        return remote(src, dst, self.ring, (direction, a, step), device)

    def spread(self, a, index, src=None):
        src = self.slot(a, index) if src is None else src
        if self.way.use_outer:
            copy = remote(src, self.slot(a, index), self.outer, (a, index), self.links.across())
            copy.start()
            self.pending.append(copy)
        if self.way.use_core:
            copy = remote(src, self.slot(a, index), self.core, (0, a, index), self.links.sibling())
            copy.start()
            self.pending.append(copy)

    def relay(self, index):
        if not self.way.use_outer:
            return
        for a in range(self.way.arrays):
            slot = self.slot(a, index, outer_flip=1)
            remote(slot, slot, self.outer, (a, index), self.links.across()).wait_recv()
            if self.way.use_core:
                copy = remote(slot, slot, self.core, (1, a, index), self.links.sibling())
                copy.start()
                self.pending.append(copy)

    def halves(self, a):
        low = self.way.splits[a]
        rows = self.own[a].shape[0]
        parts = []
        if low > 0:
            parts.append((0, pl.ds(0, low)))
        if low < rows:
            parts.append((1, pl.ds(low, rows - low)))
        return parts

    def start(self):
        for a in range(self.way.arrays):
            for direction in range(2):
                copy = self.hop(a, 0, direction, 1, src=self.own[a])
                copy.start()
                self.pending.append(copy)
        for a in range(self.way.arrays):
            self.spread(a, 0, src=self.own[a])
            copy = pltpu.make_async_copy(self.own[a], self.slot(a, 0), self.local.at[a])
            copy.start()

    def round(self, step):
        way = self.way
        if step <= way.steps:
            for a in range(way.arrays):
                for direction in range(2):
                    index = 2 * step - 1 + direction
                    self.hop(a, index, direction, step).wait_recv()
                    if step < way.steps:
                        copy = self.hop(a, index, direction, step + 1)
                        copy.start()
                        self.pending.append(copy)
                    elif len(way.distances) % 2 == 0:
                        for side, rows in self.halves(a):
                            if side == direction:
                                copy = self.hop(a, index, direction, step + 1, rows=rows)
                                copy.start()
                                self.pending.append(copy)
            for a in range(way.arrays):
                for direction in range(2):
                    self.spread(a, 2 * step - 1 + direction)
        else:
            last = len(way.distances) - 1
            for a in range(way.arrays):
                for side, rows in self.halves(a):
                    self.hop(a, last, side, step, rows=rows).wait_recv()
                self.spread(a, last)

    def rounds(self):
        return self.way.steps + (1 if len(self.way.distances) % 2 == 0 else 0)

    def tail(self):
        for index in range(max(0, 2 * self.rounds() - 3), len(self.way.distances)):
            self.relay(index)

    def finish(self):
        way = self.way
        for a in range(way.arrays):
            pltpu.make_async_copy(self.own[a], self.slot(a, 0), self.local.at[a]).wait()
        if way.use_core:
            for index in range(len(way.distances)):
                for a in range(way.arrays):
                    for o in range(way.outers):
                        slot = self.slot(a, index, outer_flip=o, core_flip=1)
                        remote(slot, slot, self.core, (o, a, index), self.links.sibling()).wait_recv()
        for copy in self.pending:
            copy.wait_send()


def gather_kernel(ways, set_sizes, tp_count, grp_count, *refs):
    links = Links(tp_count, grp_count)
    arrays = sum(way.arrays for way in ways)
    own, full, scratch = refs[:arrays], refs[arrays : 2 * arrays], refs[2 * arrays :]
    gathers, at = [], 0
    for i, way in enumerate(ways):
        gathers.append(
            Gather(way, links, own[at : at + way.arrays], full[at : at + way.arrays], scratch[7 * i : 7 * i + 7])
        )
        at += way.arrays
    links.greet(any(w.use_core for w in ways), any(w.use_outer for w in ways))
    sets, at = [], 0
    for size in set_sizes:
        sets.append(gathers[at : at + size])
        at += size
    for gather in sets[0]:
        gather.start()
    for i, group in enumerate(sets):
        rounds, steps = group[0].rounds(), group[0].way.steps
        for step in range(1, rounds + 1):
            for gather in group:
                gather.round(step)
            if step == steps and i + 1 < len(sets):
                for gather in sets[i + 1]:
                    gather.start()
            for gather in group:
                for index in [0] if step == 2 else [2 * step - 5, 2 * step - 4] if step > 2 else []:
                    gather.relay(index)
            if step == 1 and i > 0:
                for gather in sets[i - 1]:
                    gather.tail()
    for gather in sets[-1]:
        gather.tail()
    for gather in gathers:
        gather.finish()


def gather_weights(ways, set_sizes, pieces, tp_count, grp_count, collective_id):
    arrays = [x for p in pieces for x in p]
    shares = [way.shares for way in ways for _ in range(way.arrays)]
    out = pl.pallas_call(
        functools.partial(gather_kernel, ways, set_sizes, tp_count, grp_count),
        in_specs=[pl.BlockSpec(memory_space=pltpu.VMEM)] * len(arrays),
        out_specs=[pl.BlockSpec(memory_space=pltpu.HBM)] * len(arrays),
        out_shape=[
            jax.ShapeDtypeStruct((tp_count, s) + x.shape, x.dtype) for s, x in zip(shares, arrays)
        ],
        scratch_shapes=[s for way in ways for s in Gather.scratch(way)],
        compiler_params=pltpu.CompilerParams(collective_id=collective_id, has_side_effects=True),
    )(*arrays)
    return out


def sum_rows(target, terms):
    rows = target.shape[0]

    def some(span):
        total = terms[0][span, :].astype(F32)
        for term in terms[1:]:
            total = total + term[span, :].astype(F32)
        target[span, :] = total.astype(target.dtype)

    whole = rows // 16

    def step(i, carry):
        some(pl.ds(pl.multiple_of(i * 16, 16), 16))
        return carry

    lax.fori_loop(0, whole, step, 0)
    if rows % 16:
        some(pl.ds(whole * 16, rows % 16))


class Reduce:
    @staticmethod
    def scratch(way, rows, width):
        n = len(way.distances)
        shapes = []
        for a in range(way.arrays):
            shapes += [
                pltpu.VMEM((n, way.outers, rows[a], width), BF16),
                pltpu.VMEM((n if way.use_outer else 1, rows[a], width), BF16),
                pltpu.VMEM((2, way.steps + 1, rows[a], width), BF16),
                pltpu.VMEM((way.shares, rows[a], width), BF16),
                pltpu.VMEM((1, rows[a], width), BF16),
            ]
        a = way.arrays
        shapes += sem_pair(2, a, way.steps + 2) + sem_pair(a, n) + sem_pair(2, a, n)
        return shapes + sem_pair(a) + sem_pair(2, a)

    @staticmethod
    def scratch_count(way):
        return 5 * way.arrays + 10

    def __init__(self, way, links, parts, scratch):
        self.way, self.links, self.parts = way, links, parts
        bufs, sems = scratch[: 5 * way.arrays], scratch[5 * way.arrays :]
        self.acc, self.cross, self.land, self.total, self.other = (bufs[k::5] for k in range(5))
        self.ring, self.outer, self.core = sems[0:2], sems[2:4], sems[4:6]
        self.last_outer, self.last_core = sems[6:8], sems[8:10]
        self.pending = []

    def part(self, a, index, **flips):
        way = self.way
        return self.parts[a].at[self.links.shard(way.distances[index]), way.share(self.links, **flips)]

    def send(self, src, dst, sems, index, device):
        copy = remote(src, dst, sems, index, device)
        copy.start()
        self.pending.append(copy)

    def order(self):
        return list(range(len(self.way.distances)))[::-1]

    def swap(self, index):
        way = self.way
        if way.use_core:
            for o in range(way.outers)[::-1]:
                for a in range(way.arrays):
                    self.send(
                        self.part(a, index, outer_flip=o, core_flip=1),
                        self.acc[a].at[index, o], self.core, (o, a, index), self.links.sibling(),
                    )

    def wait_swap(self, a, index, o):
        if self.way.use_core:
            slot = self.acc[a].at[index, o]
            remote(slot, slot, self.core, (o, a, index), self.links.sibling()).wait_recv()

    def crossing(self, index):
        way = self.way
        if way.use_outer:
            for a in range(way.arrays):
                self.wait_swap(a, index, 1)
                slot = self.acc[a].at[index, 1]
                terms = [self.part(a, index, outer_flip=1)] + ([slot] if way.use_core else [])
                sum_rows(slot, terms)
                self.send(slot, self.cross[a].at[index], self.outer, (a, index), self.links.across())

    def terms(self, a, index):
        way = self.way
        self.wait_swap(a, index, 0)
        terms = [self.part(a, index)] + ([self.acc[a].at[index, 0]] if way.use_core else [])
        if way.use_outer:
            slot = self.cross[a].at[index]
            remote(slot, slot, self.outer, (a, index), self.links.across()).wait_recv()
            terms.append(slot)
        return terms

    def halves(self, a):
        low, rows = self.way.splits[a], self.acc[a].shape[2]
        parts = []
        if low > 0:
            parts.append((0, pl.ds(0, low)))
        if low < rows:
            parts.append((1, pl.ds(low, rows - low)))
        return parts

    def toward(self, direction):
        return self.links.down() if direction == 0 else self.links.up()

    def opposite(self):
        way = self.way
        if len(way.distances) % 2:
            return
        index = len(way.distances) - 1
        for a in range(way.arrays):
            sum_rows(self.acc[a].at[index, 0], self.terms(a, index))
            for side, rows in self.halves(a):
                self.send(
                    self.acc[a].at[index, 0].at[rows], self.land[a].at[side, way.steps].at[rows],
                    self.ring, (side, a, way.steps + 1), self.toward(side),
                )

    def wait_land(self, a, side, step, rows=None):
        slot = self.land[a].at[side, step - 1]
        if rows is not None:
            slot = slot.at[rows]
        remote(slot, slot, self.ring, (side, a, step), self.toward(side)).wait_recv()
        return slot

    def step(self, step):
        way = self.way
        for side in range(2):
            index = 2 * step - 1 + side
            for a in range(way.arrays):
                slot = self.acc[a].at[index, 0]
                terms = self.terms(a, index)
                if step < way.steps:
                    terms.append(self.wait_land(a, side, step + 1))
                    sum_rows(slot, terms)
                elif len(way.distances) % 2 == 0:
                    sum_rows(slot, terms)
                    for half, rows in self.halves(a):
                        if half == side:
                            got = self.wait_land(a, side, step + 1, rows)
                            sum_rows(slot.at[rows], [slot.at[rows], got])
                else:
                    sum_rows(slot, terms)
                self.send(
                    slot, self.land[a].at[side, step - 1], self.ring, (side, a, step), self.toward(side)
                )

    def close(self):
        way = self.way
        for a in range(way.arrays):
            terms = self.terms(a, 0) + [self.wait_land(a, side, 1) for side in range(2)]
            if way.use_core and not way.use_outer:
                slot = self.acc[a].at[0, 0]
                sum_rows(slot, terms)
                self.send(slot, self.other[a].at[0], self.last_outer, (a,), self.links.across())
            else:
                slot = self.total[a].at[way.share(self.links)]
                sum_rows(slot, terms)
                if way.use_outer:
                    self.send(slot, slot, self.last_outer, (a,), self.links.across())
                if way.use_core:
                    self.send(slot, slot, self.last_core, (0, a), self.links.sibling())

    def share_out(self):
        way = self.way
        if not way.use_core:
            return
        for a in range(way.arrays):
            if way.use_outer:
                slot = self.total[a].at[way.share(self.links, outer_flip=1)]
                remote(slot, slot, self.last_outer, (a,), self.links.across()).wait_recv()
                self.send(slot, slot, self.last_core, (1, a), self.links.sibling())
            else:
                other = self.other[a].at[0]
                remote(other, other, self.last_outer, (a,), self.links.across()).wait_recv()
                slot = self.total[a].at[way.share(self.links)]
                sum_rows(slot, [self.acc[a].at[0, 0], other])
                self.send(slot, slot, self.last_core, (0, a), self.links.sibling())

    def finish(self, outs):
        way = self.way
        if way.use_core:
            for a in range(way.arrays):
                for o in range(way.outers):
                    slot = self.total[a].at[way.share(self.links, outer_flip=o, core_flip=1)]
                    remote(slot, slot, self.last_core, (o, a), self.links.sibling()).wait_recv()
        for a in range(way.arrays):
            for share in range(way.shares):
                sum_rows(outs[a].at[share], [self.total[a].at[share]])
        for copy in self.pending:
            copy.wait_send()


def reduce_kernel(ways, tp_count, grp_count, *refs):
    links = Links(tp_count, grp_count)
    arrays = sum(way.arrays for way in ways)
    parts, outs, scratch = refs[:arrays], refs[arrays : 2 * arrays], refs[2 * arrays :]
    reduces, at, low = [], 0, 0
    for way in ways:
        count = Reduce.scratch_count(way)
        reduces.append((Reduce(way, links, parts[at : at + way.arrays], scratch[low : low + count]), outs[at : at + way.arrays]))
        at += way.arrays
        low += count
    links.greet(any(w.use_core for w in ways), True, any(w.use_core for w in ways))
    only = [r for r, _ in reduces]
    for index in only[0].order():
        for reduce in only:
            reduce.swap(index)
    for index in only[0].order():
        for reduce in only:
            reduce.crossing(index)
    for reduce in only:
        reduce.opposite()
    for step in range(only[0].way.steps, 0, -1):
        for reduce in only:
            reduce.step(step)
    for reduce in only:
        reduce.close()
    for reduce in only:
        reduce.share_out()
    for reduce, out in reduces:
        reduce.finish(out)


def reduce_weights(ways, parts, tp_count, grp_count, collective_id):
    width = parts[0].shape[-1]
    rows = [x.shape[2] for x in parts]
    scratch, at = [], 0
    for way in ways:
        scratch += Reduce.scratch(way, rows[at : at + way.arrays], width)
        at += way.arrays
    vmem = pl.BlockSpec(memory_space=pltpu.VMEM)
    return pl.pallas_call(
        functools.partial(reduce_kernel, ways, tp_count, grp_count),
        in_specs=[vmem] * len(parts),
        out_specs=[vmem] * len(parts),
        out_shape=[jax.ShapeDtypeStruct(x.shape[1:], F32) for x in parts],
        scratch_shapes=scratch,
        compiler_params=pltpu.CompilerParams(collective_id=collective_id, has_side_effects=True),
    )(*parts)


def softmax_of(q, k, key_bias):
    scores = dot(q, k, NT) * SCALE + key_bias
    exps = jnp.exp(scores - jnp.max(scores, axis=-1, keepdims=True))
    return exps / jnp.sum(exps, axis=-1, keepdims=True)


def attend_kernel(images, x_ref, qk_ref, vo_ref, qkb_ref, vb_ref, key_ref, qk_out, v_out, o_out, acc_ref):
    rows = x_ref.shape[0] // images
    x = x_ref[...]
    qk = (dot(x, qk_ref[0, 0], NT) + qkb_ref[0, 0]).astype(BF16)
    v = (dot(x, vo_ref[0, 0, 0], NT) + vb_ref[0, 0]).astype(BF16)
    qk_out[0, 0] = qk
    v_out[0, 0] = v
    for image in range(images):
        span = slice(image * rows, (image + 1) * rows)
        probs = softmax_of(qk[span, :HEAD_DIM], qk[span, HEAD_DIM:], key_ref[image])
        o_out[0, 0, span, :] = dot(probs.astype(BF16), v[span], NN).astype(BF16)
    update = dot(o_out[0, 0], vo_ref[0, 1, 0], NN)

    @pl.when(pl.program_id(0) == 0)
    def _():
        acc_ref[...] = update

    @pl.when(pl.program_id(0) > 0)
    def _():
        acc_ref[...] += update


def head_specs(local):
    whole = lambda *shape: pl.BlockSpec(shape, lambda h: (0,) * len(shape))
    per_head = lambda *shape: pl.BlockSpec(
        (1, 1) + shape, lambda h: (h // local, h % local) + (0,) * len(shape)
    )
    pair = lambda *shape: pl.BlockSpec(
        (1, 2, 1) + shape, lambda h: (h // local, 0, h % local) + (0,) * len(shape)
    )
    return whole, per_head, pair


def attend(attn_in, w_qk, w_vo, qk_bias, v_bias, key_bias):
    shards, local, _, width = w_qk.shape
    rows = attn_in.shape[0]
    images, _, cap = key_bias.shape
    whole, per_head, pair = head_specs(local)
    return pl.pallas_call(
        functools.partial(attend_kernel, images),
        grid=(shards * local,),
        in_specs=[
            whole(rows, width),
            per_head(2 * HEAD_DIM, width),
            pair(HEAD_DIM, width),
            per_head(1, 2 * HEAD_DIM),
            per_head(1, HEAD_DIM),
            whole(images, 1, cap),
        ],
        out_specs=[
            per_head(rows, 2 * HEAD_DIM),
            per_head(rows, HEAD_DIM),
            per_head(rows, HEAD_DIM),
            whole(rows, width),
        ],
        out_shape=[
            jax.ShapeDtypeStruct((shards, local, rows, 2 * HEAD_DIM), BF16),
            jax.ShapeDtypeStruct((shards, local, rows, HEAD_DIM), BF16),
            jax.ShapeDtypeStruct((shards, local, rows, HEAD_DIM), BF16),
            jax.ShapeDtypeStruct((rows, width), F32),
        ],
    )(attn_in, w_qk, w_vo, qk_bias, v_bias, key_bias)


def attend_back_kernel(
    images, x_ref, grad_ref, qkw_ref, vow_ref, qk_ref, v_ref, o_ref, key_ref,
    dqkw_ref, dvow_ref, dqkb_ref, dvb_ref, dx_ref, dqk_ref, dv_ref,
):
    rows = x_ref.shape[0] // images
    grad_out = dot(grad_ref[...], vow_ref[0, 1, 0], NT).astype(BF16)
    for image in range(images):
        span = slice(image * rows, (image + 1) * rows)
        q, k = qk_ref[0, 0, span, :HEAD_DIM], qk_ref[0, 0, span, HEAD_DIM:]
        probs = softmax_of(q, k, key_ref[image])
        gout = grad_out[span]
        grad_probs = dot(gout, v_ref[0, 0, span, :], NT)
        inner = jnp.sum(probs * grad_probs, axis=-1, keepdims=True)
        grad_scores = (probs * (grad_probs - inner)).astype(BF16)
        dqk_ref[span, :HEAD_DIM] = (dot(grad_scores, k, NN) * SCALE).astype(BF16)
        dqk_ref[span, HEAD_DIM:] = (dot(grad_scores, q, TN) * SCALE).astype(BF16)
        dv_ref[span, :] = dot(probs.astype(BF16), gout, TN).astype(BF16)

    dqk, dv, x = dqk_ref[...], dv_ref[...], x_ref[...]
    dqkw_ref[0, 0] = dot(dqk, x, TN).astype(BF16)
    dvow_ref[0, 0, 0] = dot(dv, x, TN).astype(BF16)
    dvow_ref[0, 1, 0] = dot(o_ref[0, 0], grad_ref[...], TN).astype(BF16)
    dqkb_ref[0, 0] = jnp.sum(dqk.astype(F32), axis=0, keepdims=True)
    dvb_ref[0, 0] = jnp.sum(dv.astype(F32), axis=0, keepdims=True)
    update = dot(dqk, qkw_ref[0, 0], NN) + dot(dv, vow_ref[0, 0, 0], NN)

    @pl.when(pl.program_id(0) == 0)
    def _():
        dx_ref[...] = update

    @pl.when(pl.program_id(0) > 0)
    def _():
        dx_ref[...] += update


def attend_back(attn_in, grad_rows, w_qk, w_vo, qk, v, attn_out, key_bias):
    shards, local, _, width = w_qk.shape
    rows = attn_in.shape[0]
    images, _, cap = key_bias.shape
    whole, per_head, pair = head_specs(local)
    return pl.pallas_call(
        functools.partial(attend_back_kernel, images),
        grid=(shards * local,),
        in_specs=[
            whole(rows, width),
            whole(rows, width),
            per_head(2 * HEAD_DIM, width),
            pair(HEAD_DIM, width),
            per_head(rows, 2 * HEAD_DIM),
            per_head(rows, HEAD_DIM),
            per_head(rows, HEAD_DIM),
            whole(images, 1, cap),
        ],
        out_specs=[
            per_head(2 * HEAD_DIM, width),
            pair(HEAD_DIM, width),
            per_head(1, 2 * HEAD_DIM),
            per_head(1, HEAD_DIM),
            whole(rows, width),
        ],
        out_shape=[
            jax.ShapeDtypeStruct((shards, local, 2 * HEAD_DIM, width), BF16),
            jax.ShapeDtypeStruct((shards, 2, local, HEAD_DIM, width), BF16),
            jax.ShapeDtypeStruct((shards, local, 1, 2 * HEAD_DIM), F32),
            jax.ShapeDtypeStruct((shards, local, 1, HEAD_DIM), F32),
            jax.ShapeDtypeStruct((rows, width), F32),
        ],
        scratch_shapes=[pltpu.VMEM((rows, 2 * HEAD_DIM), BF16), pltpu.VMEM((rows, HEAD_DIM), BF16)],
    )(attn_in, grad_rows, w_qk, w_vo, qk, v, attn_out, key_bias)


def layer_stats(values):
    centred = values - jnp.mean(values, axis=-1, keepdims=True)
    inv_std = lax.rsqrt(jnp.mean(centred * centred, axis=-1, keepdims=True) + 1e-06)
    return (centred * inv_std, inv_std)


def layer_back(grad_norm, normed, inv_std):
    mean_grad = jnp.mean(grad_norm, axis=-1, keepdims=True)
    mean_proj = jnp.mean(grad_norm * normed, axis=-1, keepdims=True)
    return inv_std * (grad_norm - mean_grad - normed * mean_proj)


def gelu_both(values):
    coef = (2.0 / jnp.pi) ** 0.5
    square = values * values
    tanh = jnp.tanh(coef * values * (1.0 + 0.044715 * square))
    act = 0.5 * values * (1.0 + tanh)
    slope = 0.5 * (1.0 + tanh) + 0.5 * values * (1.0 - tanh * tanh) * coef * (
        1.0 + 3 * 0.044715 * square
    )
    return act, slope


def shift_grp(x, shift, count):
    return lax.ppermute(x, "grp", [((g + shift) % count, g) for g in range(count)])


def body(
    tokens, cond, keep_counts, orders, ada_weight, ada_bias, qkv_weight, qv_bias,
    out_weight, out_bias, fc1_weight, fc1_bias, fc2_weight, fc2_bias, cotangent,
):
    tp_rank = lax.axis_index("tp")
    grp_rank = lax.axis_index("grp")
    tp_count = lax.axis_size("tp")
    grp_count = lax.axis_size("grp")
    img_dev, tok_count, width = tokens.shape
    img_group = cond.shape[0]
    part = width // tp_count
    hidden = fc1_bias.shape[0]
    local = part // HEAD_DIM
    cap = 3 * tok_count // 4
    row_count = img_dev * cap

    split = grp_count == 4 and local % 2 == 0
    own_b = local // 2 if split else local
    rows_b = hidden * 4 // 9
    rows_x = hidden - rows_b
    if split:
        rows_b, rows_x = rows_b // 2, rows_x // 4
    way = lambda outer, low: Way(tp_count, grp_count, split, split and outer, [low])
    head_ways = [way(True, own_b * HEAD_DIM // 32 * 16), way(False, own_b * 5 * HEAD_DIM // 72 * 16)]
    ff_ways = [way(True, rows_x // 32 * 16), way(False, rows_b * 5 // 128 * 16)]
    share_x = grp_rank if split else 0
    share_b = grp_rank % 2 if split else 0
    pick = lambda x, share: lax.dynamic_index_in_dim(x, share, 0, keepdims=False)

    qkv_rows = qkv_weight.reshape(width, 3, part)
    vo = jnp.stack([qkv_rows[:, 2].T, out_weight]).reshape(-1, 2 * part // head_ways[0].shares, width)
    qk = qkv_rows[:, :2].reshape(width, 2, local, HEAD_DIM).transpose(2, 1, 3, 0)
    qk = qk.reshape(head_ways[1].shares, -1, width)
    ff_x = rows_x * ff_ways[0].shares
    pieces = [[pick(vo, share_x)], [pick(qk, share_b)]]
    for weight in (fc1_weight.T, fc2_weight):
        pieces.append([pick(weight[:ff_x].reshape(-1, rows_x, width), share_x)])
        pieces.append([pick(weight[ff_x:].reshape(-1, rows_b, width), share_b)])
    if split:
        gathered = gather_weights(
            head_ways + ff_ways + ff_ways, [2, 2, 2], pieces, tp_count, grp_count, 0
        )
    else:
        gathered = [lax.all_gather(x[None], "tp") for p in pieces for x in p]
    w_vo, w_qk, w1x, w1b, w2x, w2b = gathered
    w_vo = w_vo.reshape(tp_count, 2, local, HEAD_DIM, width)
    w_qk = w_qk.reshape(tp_count, local, 2 * HEAD_DIM, width)
    flat = lambda x: x.reshape(-1, width)

    own_orders = lax.dynamic_slice_in_dim(orders, tp_rank * img_dev, img_dev, 0)[:, :cap]
    own_counts = lax.dynamic_slice_in_dim(keep_counts, tp_rank * img_dev, img_dev, 0)
    slot = lax.broadcasted_iota(jnp.int32, (img_dev, cap), 1)
    kept = slot < own_counts[:, None]
    place_ids = lax.broadcasted_iota(jnp.int32, (1, 1, tok_count), 2)
    chosen = ((own_orders[:, :, None] == place_ids) & kept[:, :, None]).astype(BF16)
    take = lambda x: jnp.einsum("ijt,itd->ijd", chosen, x, preferred_element_type=F32)
    put = lambda x: jnp.einsum("ijt,ijd->itd", chosen, x.astype(BF16), preferred_element_type=F32)
    key_bias = jnp.where(kept, 0.0, -1e30).astype(F32)[:, None, :]
    keep_col = kept.astype(F32)[:, :, None]

    silu_cond = jax.nn.silu(cond.astype(F32)).astype(BF16)
    ada_cols = (
        jnp.einsum("id,dke->ike", silu_cond, ada_weight, preferred_element_type=F32)
        + ada_bias.astype(F32)[None]
    )
    biases = jnp.concatenate([fc1_bias, qv_bias.reshape(-1)]).astype(F32)
    mod_len = img_dev * 6 * part
    message = jnp.concatenate(
        [
            ada_cols.reshape(tp_count, mod_len),
            jnp.broadcast_to(biases[None], (tp_count, biases.shape[0])),
        ],
        axis=1,
    )
    message = lax.all_to_all(message, "tp", split_axis=0, concat_axis=0, tiled=True)
    modulation = message[:, :mod_len].reshape(tp_count, img_dev, 6, part)
    modulation = modulation.transpose(1, 2, 0, 3).reshape(img_dev, 6, width)
    shift_one, scale_one, gate_one, shift_two, scale_two, gate_two = (
        modulation[:, j][:, None, :] for j in range(6)
    )
    b1 = message[:, mod_len : mod_len + hidden]
    b1x, b1b = b1[:, :ff_x].reshape(-1, 1), b1[:, ff_x:].reshape(-1, 1)
    qv = message[:, mod_len + hidden :].reshape(tp_count, 2, local, 1, HEAD_DIM)
    qk_bias = jnp.concatenate([qv[:, 0], jnp.zeros_like(qv[:, 0])], axis=-1)
    v_bias = qv[:, 1]

    resid = take(tokens)
    grad_out = take(cotangent)
    normed_one, inv_one = layer_stats(resid)
    attn_in = (normed_one * (1.0 + scale_one) + shift_one).astype(BF16).reshape(row_count, width)
    qk, v, attn_out, branch_one = attend(attn_in, w_qk, w_vo, qk_bias, v_bias, key_bias)
    branch_one = branch_one.reshape(img_dev, cap, width) + out_bias.astype(F32)
    delta_one = keep_col * gate_one * branch_one
    hidden_res = resid + delta_one
    normed_two, inv_two = layer_stats(hidden_res)
    mlp_in = (normed_two * (1.0 + scale_two) + shift_two).astype(BF16).reshape(row_count, width)
    grad_two = (grad_out * gate_two).astype(BF16).reshape(row_count, width)
    halves = [(w1x, w2x, b1x), (w1b, w2b, b1b)]
    acts, slopes = [], []
    for w1, _, bias in halves:
        act, slope = gelu_both(dot(flat(w1), mlp_in, NT) + bias)
        acts.append(act.astype(BF16))
        slopes.append(slope.astype(BF16))
    branch_two = sum(dot(act, flat(w2), TN) for act, (_, w2, _) in zip(acts, halves))
    branch_two = branch_two.reshape(img_dev, cap, width) + fc2_bias.astype(F32)
    delta_two = keep_col * gate_two * branch_two
    block_out = tokens.astype(F32) + put(delta_one + delta_two)
    gate_grad_two = jnp.sum(grad_out * branch_two, axis=1)

    ff_parts, grads_pre = [], []
    for act, slope, (w1, w2, _) in zip(acts, slopes, halves):
        grad_pre = (dot(flat(w2), grad_two, NT) * slope.astype(F32)).astype(BF16)
        grads_pre.append(grad_pre)
        ff_parts.append(dot(act, grad_two, NN).astype(BF16).reshape(w2.shape))
    for grad_pre, (w1, _, _) in zip(grads_pre, halves):
        ff_parts.append(dot(grad_pre, mlp_in, NN).astype(BF16).reshape(w1.shape))
    fc1b_part = jnp.concatenate(
        [jnp.sum(g.astype(F32), axis=1).reshape(tp_count, -1) for g in grads_pre], axis=1
    )
    fc2b_part = jnp.sum(grad_two.astype(F32), axis=0)
    grad_mlp_in = sum(dot(g, flat(w1), TN) for g, (w1, _, _) in zip(grads_pre, halves))
    grad_mlp_in = grad_mlp_in.reshape(img_dev, cap, width)
    shift_grad_two = jnp.sum(grad_mlp_in, axis=1)
    scale_grad_two = jnp.sum(grad_mlp_in * normed_two, axis=1)
    back_two = layer_back(grad_mlp_in * (1.0 + scale_two), normed_two, inv_two)
    grad_hidden = grad_out + back_two
    gate_grad_one = jnp.sum(grad_hidden * keep_col * branch_one, axis=1)
    grad_one = (grad_hidden * keep_col * gate_one).astype(BF16).reshape(row_count, width)
    outb_part = jnp.sum(grad_one.astype(F32), axis=0)
    dqk, dvo, dqk_bias, dv_bias, grad_attn_in = attend_back(
        attn_in, grad_one, w_qk, w_vo, qk, v, attn_out, key_bias
    )
    head_parts = [
        dvo.reshape(tp_count, head_ways[0].shares, -1, width),
        dqk.reshape(tp_count, head_ways[1].shares, -1, width),
    ]
    if split:
        ff_sums = reduce_weights(ff_ways + ff_ways, ff_parts, tp_count, grp_count, 1)
        head_sums = reduce_weights(head_ways, head_parts, tp_count, grp_count, 2)
    else:
        scatter = lambda x: lax.psum_scatter(x, "tp", scatter_dimension=0)
        ff_sums, head_sums = (
            [lax.psum(scatter(x), "grp").astype(F32) for x in parts]
            for parts in (ff_parts, head_parts)
        )
    fc2_sum = jnp.concatenate([flat(ff_sums[0]), flat(ff_sums[1])])
    fc1_sum = jnp.concatenate([flat(ff_sums[2]), flat(ff_sums[3])])
    v_sum, out_sum = flat(head_sums[0])[:part], flat(head_sums[0])[part:]
    qk_sum = head_sums[1].reshape(local, 2, HEAD_DIM, width).transpose(1, 0, 2, 3)
    qkv_sum = jnp.concatenate([qk_sum.reshape(2, part, width), v_sum[None]]).transpose(2, 0, 1)

    grad_attn_in = grad_attn_in.reshape(img_dev, cap, width)
    shift_grad_one = jnp.sum(grad_attn_in, axis=1)
    scale_grad_one = jnp.sum(grad_attn_in * normed_one, axis=1)
    back_one = layer_back(grad_attn_in * (1.0 + scale_one), normed_one, inv_one)
    grad_tokens = cotangent.astype(F32) + put(back_two + back_one)

    modulation_grad = jnp.stack(
        [
            shift_grad_one, scale_grad_one, gate_grad_one,
            shift_grad_two, scale_grad_two, gate_grad_two,
        ],
        axis=1,
    )
    mod_rows = modulation_grad.reshape(img_dev, 6, tp_count, part).transpose(2, 0, 1, 3)
    message = jnp.concatenate(
        [
            mod_rows.reshape(tp_count, mod_len),
            fc1b_part,
            dqk_bias[..., :HEAD_DIM].reshape(tp_count, part),
            dv_bias.reshape(tp_count, part),
            outb_part.reshape(tp_count, part),
            fc2b_part.reshape(tp_count, part),
        ],
        axis=1,
    )
    message = lax.all_to_all(message, "tp", split_axis=0, concat_axis=0, tiled=True)
    grad_cols = message[:, :mod_len].reshape(img_group, 6, part).astype(BF16)
    bias_sums = jnp.sum(message[:, mod_len:], axis=0)
    shifts = range(1, grp_count)
    around = lambda x: [x] + [shift_grp(x, k, grp_count) for k in shifts]
    cols_all = jnp.concatenate(around(grad_cols), 0)
    silu_all = jnp.concatenate(around(silu_cond), 0)
    bias_sums = sum(around(bias_sums))
    kept_int = jnp.sum(sum(around(keep_counts)))
    kept_total = kept_int.astype(F32)
    ada_sum = jnp.einsum("id,ike->dke", silu_all, cols_all, preferred_element_type=F32)
    adab_sum = jnp.sum(cols_all.astype(F32), axis=0)
    cond_part = jnp.einsum("ike,dke->id", grad_cols, ada_weight, preferred_element_type=F32)
    cond_part = cond_part.astype(BF16).reshape(img_group, tp_count, part).transpose(1, 0, 2)
    cond_rows = lax.all_to_all(
        cond_part.reshape(tp_count, img_group * part), "tp", split_axis=0, concat_axis=0, tiled=True
    )
    cond_sum = jnp.sum(cond_rows.astype(F32), axis=0).reshape(img_group, part)
    cond_cols = lax.dynamic_slice_in_dim(cond, tp_rank * part, part, 1).astype(F32)
    cond_grad = jax.vjp(jax.nn.silu, cond_cols)[1](cond_sum)[0]

    all_tokens = img_group * tok_count * grp_count
    token_counts = jnp.stack([kept_int, all_tokens - kept_int]).astype(jnp.int32)
    at = [0, hidden, hidden + 2 * part, hidden + 3 * part, hidden + 4 * part]
    fc1b_sum, qvb_sum, outb_sum, fc2b_sum = (bias_sums[a:b] for a, b in zip(at, at[1:]))
    scaled = lambda x: x.astype(F32) / kept_total
    return (
        block_out,
        grad_tokens,
        cond_grad,
        scaled(ada_sum),
        scaled(adab_sum),
        scaled(qkv_sum),
        scaled(qvb_sum.reshape(2, part)),
        scaled(out_sum),
        scaled(outb_sum),
        scaled(fc1_sum.T),
        scaled(fc1b_sum),
        scaled(fc2_sum),
        scaled(fc2b_sum),
        token_counts,
    )


def solution(mesh):
    in_specs = (
        P(("grp", "tp"), None, None),
        P("grp", None),
        P("grp"),
        P("grp", None),
        P(None, None, "tp"),
        P(None, "tp"),
        P(None, None, "tp"),
        P(None, "tp"),
        P("tp", None),
        P(),
        P(None, "tp"),
        P("tp"),
        P("tp", None),
        P(),
        P(("grp", "tp"), None, None),
    )
    out_specs = (
        P(("grp", "tp"), None, None),
        P(("grp", "tp"), None, None),
        P("grp", "tp"),
        P(None, None, "tp"),
        P(None, "tp"),
        P(None, None, "tp"),
        P(None, "tp"),
        P("tp", None),
        P("tp"),
        P(None, "tp"),
        P("tp"),
        P("tp", None),
        P("tp"),
        P(),
    )
    return jax.shard_map(body, mesh=mesh, in_specs=in_specs, out_specs=out_specs, check_vma=False)
```

time: 1870 us -> 567 us (0.30)
  waiting for transfers between devices: 1570 us -> 2.37 us
  Pallas kernels: 0 us -> 386 us
  matrix products: 148 us -> 76.4 us
  other arithmetic: 71.5 us -> 35.6 us
    reduce_scatter x4 -> x0, waiting for transfers between devices: 877 us -> none  [the longest x1 306 us: body(): lax.psum_scatter(jnp.dot(attn_out, out_use, preferred_element_type=WIDE_T...]
    all_gather x4 -> x0, waiting for transfers between devices: 532 us -> none  [the longest x1 136 us: body(): grad_rows_one = lax.all_gather(branch_grad_one, 'tp', axis=0, tiled=True)]
    pallas_call x0 -> x5, Pallas kernels: none -> 386 us  [the longest x2 182 us: reduce_weights(): pl.pallas_call(functools.partial(reduce_kernel, ways, tp_count, grp_count...]
    psum x1 -> x0, waiting for transfers between devices: 116 us -> none  [body(): lax.psum(ada_grad.astype(jnp.bfloat16), 'grp').astype(jnp.float32)]
    dot_general x19, matrix products: 134 us -> 76.4 us  [the longest x12 60.1 us: dot(): return lax.dot_general(a, b, dims, preferred_element_type=F32)]
    unnamed x11 -> x0, waiting for transfers between devices: 34.6 us -> none
    reduce_sum x8 -> x6, other arithmetic: 23.4 us -> 3.92 us  [the longest x1 1.75 us: body(): outb_part = jnp.sum(grad_one.astype(F32), axis=0)]
  transfers between devices with their start and end apart: 12 -> 15, of which waited for: 11 -> 1; matrix products, arithmetic and copies ran while one was open for 5% -> 24% of each run, Pallas kernels for 0% -> 69%
where the time goes in v1:
time: 567 us; the launch traced here: 557 us
  Pallas kernels  386 us (68%)
  matrix products  76.4 us (13%)
  other arithmetic  35.6 us (6%)
  local copies, waits for them, and re-layouts  28.3 us (5%)
  starting transfers between devices  24.8 us (4%)
    pallas_call x2, Pallas kernels, reduce_weights(): pl.pallas_call(functools.partial(reduce_kernel, ways, tp_count, grp_count...  182 us
    pallas_call x1, Pallas kernels, gather_weights(): pl.pallas_call(functools.partial(gather_kernel, ways, set_sizes, tp_count...  123 us
    dot_general x12, matrix products, dot(): return lax.dot_general(a, b, dims, preferred_element_type=F32)  60.1 us
    pallas_call x1, Pallas kernels, attend_back(): pl.pallas_call(functools.partial(attend_back_kernel, images), grid=(shard...  50 us
    pallas_call x1, Pallas kernels, attend(): pl.pallas_call(functools.partial(attend_kernel, images), grid=(shards * l...  30.9 us
  transfers between devices with their start and end apart: 15, of which 1 were waited for; matrix products, arithmetic and copies ran while one was open for 24% of the time, Pallas kernels for 69%

profile of v1, /device:TPU:0, one launch (start us, length us, event | category | flops | bytes accessed | tf_op | source)
XLA Modules:
  0.0 556.7 jit_solution(5362142138258891797)
XLA Ops:
  0.7 2.5 collective-permute-start.6
  10.5 5.8 %all-to-all-start = ((f32[8,1,2592]{2,1,0:T(1,128)}), f32[8,1,2592]{2,1,0:T(1,128)S(1)}, u32[]{:S(2)}, u32[]{:S(2)}) async-start(f32[8,1,2592]{2,1,0:T(1,128)} %copy.57), calls=%async_computation | async-start | bytes 172032 | tf_op jit(solution)/shard_map/all_to_all | solution.py:758
  18.8 2.0 slice.104
  23.4 2.0 copy.59
  32.8 123.5 %shard_map.254 = (bf16[8,4,72,1152]{3,2,1,0:T(8,128)(2,1)}, bf16[8,2,144,1152]{3,2,1,0:T(8,128)(2,1)}, bf16[8,4,80,1152]{3,2,1,0:T(8,128)(2,1)}, bf16[8,2,128,11...) custom-call(bf16[72,1152]{1,0:T(8,128)(2,1)} %dynamic-slice_bitcast_fusion.5.refs_0_, ...), custom_call_target="tpu_custom_call" | custom-call | tf_op jit(solution)/shard_map/pallas_call | solution.py:258
  162.1 2.8 add_convert_fusion.5
  164.8 30.9 %shard_map.255 = (bf16[8,2,384,144]{3,2,1,0:T(8,128)(2,1)}, bf16[8,2,384,72]{3,2,1,0:T(8,128)(2,1)}, bf16[8,2,384,72]{3,2,1,0:T(8,128)(2,1)}, f32[384,1152]{1,0:T(8,128)}) custom-call(bf16[384,1152]{1,0:T(8,128)(2,1)} %bitcast.155, bf16[8,2,144,1152]{3,2,1,0:T(8,128)(2,1)} %get-tuple-element.35.qk_ref.qkw_ref, bf16[8,2,2,72,1152]{4,3,2,1,0:T(8,128)(2,1)} %bitcast.146, ...), custom_call_target="tpu_custom_call" | custom-call | tf_op jit(solution)/shard_map/pallas_call | solution.py:560
  195.7 2.4 fusion.54
  202.2 5.4 convolution_add_fusion
  207.6 4.7 fusion.53
  212.2 4.8 convert_reduce_fusion
  217.1 5.6 %convolution_convert_fusion.1 = bf16[2560,1152]{1,0:T(8,128)(2,1)} fusion(bf16[384,1152]{1,0:T(8,128)(2,1)S(1)} %bitcast.190, f32[2560,384]{0,1:T(8,128)S(1)} %convolution_add_fusion), kind=kOutput, calls=%fused_computation.1 | convolution fusion | flops 2276720640 | bytes 10715136 | tf_op jit(solution)/shard_map/dot_general | solution.py:20
  222.7 3.9 fusion.59
  226.6 5.3 convolution_convert_fusion
  232.0 4.7 fusion.58
  236.8 4.9 convolution_convert_fusion.3
  241.7 5.2 convert_reduce_fusion.1
  247.5 7.6 %convolution_add_fusion.4 = f32[384,1152]{1,0:T(8,128)} fusion(f32[384,1152]{1,0:T(8,128)} %fusion.53, bf16[2048,1152]{1,0:T(8,128)(2,1)} %bitcast.218, f32[2048,384]{0,1:T(8,128)} %copy-done.35, f32[2048]{0:T(1024)S(1)} %bitcast.209), kind=kOutput, calls=%fused_computation.20 | convolution fusion | flops 1820246016 | bytes 11411456 | tf_op jit(solution)/shard_map/dot_general | solution.py:20
  255.2 4.5 convolution_convert_fusion.2
  259.7 3.4 fusion.5
  263.3 2.8 multiply_reduce_fusion.1
  266.4 3.8 convolution_add_fusion.2
  273.3 50.0 %shard_map.256 = (bf16[8,2,144,1152]{3,2,1,0:T(8,128)(2,1)}, bf16[8,2,2,72,1152]{4,3,2,1,0:T(8,128)(2,1)}, f32[8,2,1,144]{3,2,1,0:T(1,128)}, f32[8,2,1,72]{3,2,1,0:T(1,128)}, f32[384,1152]{1,0:T(8,128)}) custom-call(bf16[384,1152]{1,0:T(8,128)(2,1)} %bitcast.156, bf16[384,1152]{1,0:T(8,128)(2,1)} %bitcast.169, ...), custom_call_target="tpu_custom_call" | custom-call | tf_op jit(solution)/shard_map/pallas_call | solution.py:626
  328.8 2.7 multiply_reduce_fusion.3
  332.8 4.5 all-to-all-start.1
  337.3 68.2 %shard_map.257 = (f32[4,72,1152]{2,1,0:T(8,128)}, f32[2,144,1152]{2,1,0:T(8,128)}) custom-call(bf16[8,4,72,1152]{3,2,1,0:T(8,128)(2,1)} %bitcast.161, bf16[8,2,144,1152]{3,2,1,0:T(8,128)(2,1)} %get-tuple-element.49.refs_1_), custom_call_target="tpu_custom_call" | custom-call | tf_op jit(solution)/shard_map/pallas_call | solution.py:506
  407.5 4.9 convolution_add_fusion.1
  413.5 113.7 %shard_map.258 = (f32[4,80,1152]{2,1,0:T(8,128)}, f32[2,128,1152]{2,1,0:T(8,128)}, f32[4,80,1152]{2,1,0:T(8,128)}, f32[2,128,1152]{2,1,0:T(8,128)}) custom-call(bf16[8,4,80,1152]{3,2,1,0:T(8,128)(2,1)} %bitcast.159, bf16[8,2,128,1152]{3,2,1,0:T(8,128)(2,1)} %bitcast.167, bf16[8,4,80,1152]{3,2,1,0:T(8,128)(2,1)} %bitcast.160, bf16[8,2,128,1152]{3,2,1,0:T(8,128)(2,1)} %bitcast.168), custom_call_target="tpu_custom_call" | custom-call | tf_op jit(solution)/shard_map/pallas_call | solution.py:506
  527.3 3.6 fusion.1
  539.5 3.8 all-to-all-start.2
  548.4 2.3 collective-permute-done.5
  550.8 3.5 convolution_divide_fusion
  (234 shorter events, 58.0 us)
Async XLA Ops:
  0.6 7.3 %copy-start = (bf16[1152,6,144]{0,2,1:T(8,128)(2,1)S(1)}, bf16[1152,6,144]{0,2,1:T(8,128)(2,1)}, u32[]{:S(2)}) copy-start(bf16[1152,6,144]{0,2,1:T(8,128)(2,1)} %param.19) | copy-start | bytes 5971972
  0.7 15.7 %copy-start.34 = (s32[16]{0:T(128)S(1)}, s32[16]{0:T(128)}, u32[]{:S(2)}) copy-start(s32[16]{0:T(128)} %param.17) | copy-start | bytes 196
  0.7 8.9 %copy-start.33 = (bf16[576]{0:T(1024)(128)(2,1)S(1)}, bf16[576]{0:T(1024)(128)(2,1)}, u32[]{:S(2)}) copy-start(bf16[576]{0:T(1024)(128)(2,1)} %param.26) | copy-start | bytes 3460
  0.7 155.7 %collective-permute-start.6 = (s32[16]{0:T(128)}, s32[16]{0:T(128)}, u32[]{:S(2)}, u32[]{:S(2)}) collective-permute-start(s32[16]{0:T(128)} %param.17), channel_id=1, source_target_pairs={{8,0},{16,8},{24,16},{0,24},{9,1},{17,9},{25,17},{1,25},{10,2},{18... | collective-permute-start | bytes 200 | tf_op jit(solution)/shard_map/ppermute | solution.py:681
  3.2 153.2 %collective-permute-start.8 = (s32[16]{0:T(128)}, s32[16]{0:T(128)}, u32[]{:S(2)}, u32[]{:S(2)}) collective-permute-start(s32[16]{0:T(128)} %param.17), channel_id=1, source_target_pairs={{24,0},{0,8},{8,16},{16,24},{25,1},{1,9},{9,17},{17,25},{26,2},{2,... | collective-permute-start | bytes 200 | tf_op jit(solution)/shard_map/ppermute | solution.py:681
  3.2 153.2 %collective-permute-start.7 = (s32[16]{0:T(128)}, s32[16]{0:T(128)}, u32[]{:S(2)}, u32[]{:S(2)}) collective-permute-start(s32[16]{0:T(128)} %param.17), channel_id=1, source_target_pairs={{16,0},{24,8},{0,16},{8,24},{17,1},{25,9},{1,17},{9,25},{18,2},{26... | collective-permute-start | bytes 200 | tf_op jit(solution)/shard_map/ppermute | solution.py:681
  5.0 545.8 %collective-permute-start.2 = (bf16[16,1152]{1,0:T(8,128)(2,1)S(1)}, bf16[16,1152]{1,0:T(8,128)(2,1)}, u32[]{:S(2)}, u32[]{:S(2)}) collective-permute-start(bf16[16,1152]{1,0:T(8,128)(2,1)S(1)} %fusion.41), channel_id=1, source_target_pairs={{24,0},{0,8},{8,16},{16,24},{25,1},{1,9},{9,17},{17,25},{26,2},{2,... | collective-permute-start | bytes 110600 | tf_op jit(solution)/shard_map/ppermute | solution.py:681
  5.9 544.9 %collective-permute-start.1 = (bf16[16,1152]{1,0:T(8,128)(2,1)S(1)}, bf16[16,1152]{1,0:T(8,128)(2,1)}, u32[]{:S(2)}, u32[]{:S(2)}) collective-permute-start(bf16[16,1152]{1,0:T(8,128)(2,1)S(1)} %fusion.41), channel_id=1, source_target_pairs={{16,0},{24,8},{0,16},{8,24},{17,1},{25,9},{1,17},{9,25},{18,2},{26... | collective-permute-start | bytes 110600 | tf_op jit(solution)/shard_map/ppermute | solution.py:681
  9.4 11.4 %copy-start.17 = (bf16[1152,576]{0,1:T(8,128)(2,1)S(1)}, bf16[1152,576]{0,1:T(8,128)(2,1)}, u32[]{:S(2)}) copy-start(bf16[1152,576]{0,1:T(8,128)(2,1)} %param.25) | copy-start | bytes 3981316
  10.5 149.7 %all-to-all-start = ((f32[8,1,2592]{2,1,0:T(1,128)}), f32[8,1,2592]{2,1,0:T(1,128)S(1)}, u32[]{:S(2)}, u32[]{:S(2)}) async-start(f32[8,1,2592]{2,1,0:T(1,128)} %copy.57), calls=%async_computation | async-start | bytes 172032 | tf_op jit(solution)/shard_map/all_to_all | solution.py:758
  17.1 181.4 %copy-start.26 = (pred[2,192]{1,0:T(4,128)(4,1)}, pred[2,192]{1,0:T(4,128)(4,1)S(1)}, u32[]{:S(2)}) copy-start(pred[2,192]{1,0:T(4,128)(4,1)S(1)} %get-tuple-element.86) | copy-start | bytes 1156
  27.5 134.5 %copy-start.24 = (f32[2,192]{1,0:T(2,128)}, f32[2,192]{1,0:T(2,128)S(1)}, u32[]{:S(2)}) copy-start(f32[2,192]{1,0:T(2,128)S(1)} %add_rsqrt_fusion.1) | copy-start | bytes 4612
  201.8 15.3 %copy-start.21 = (bf16[2,192,1152]{2,1,0:T(8,128)(2,1)}, bf16[2,192,1152]{2,1,0:T(8,128)(2,1)S(1)}, u32[]{:S(2)}) copy-start(bf16[2,192,1152]{2,1,0:T(8,128)(2,1)S(1)} %get-tuple-element.67) | copy-start | bytes 2654212
  201.8 5.8 %slice-start.6 = ((s8[5898240]{0:T(1024)(128)(4,1)}), s8[4194304]{0:T(1024)(128)(4,1)S(1)}, s32[]{:S(2)}) async-start(s8[5898240]{0:T(1024)(128)(4,1)} %bitcast.214), calls=%async_computation.9 | async-start | bytes 8388608
  202.2 5.4 slice-start.7
  207.6 15.1 %slice-start.4 = ((s8[5898240]{0:T(1024)(128)(4,1)}), s8[4194304]{0:T(1024)(128)(4,1)S(1)}, s32[]{:S(2)}) async-start(s8[5898240]{0:T(1024)(128)(4,1)} %bitcast.211), calls=%async_computation.7 | async-start | bytes 8388608
  212.2 10.5 %slice-start.5 = ((s8[5898240]{0:T(1024)(128)(4,1)}), s8[1703936]{0:T(1024)(128)(4,1)S(1)}, s32[]{:S(2)}) async-start(s8[5898240]{0:T(1024)(128)(4,1)} %bitcast.211), calls=%async_computation.8 | async-start | bytes 3407872
  232.0 9.7 %slice-start.8 = ((s8[4718592]{0:T(1024)(128)(4,1)}), s8[4194304]{0:T(1024)(128)(4,1)S(1)}, s32[]{:S(2)}) async-start(s8[4718592]{0:T(1024)(128)(4,1)} %bitcast.219), calls=%async_computation.11 | async-start | bytes 8388608
  236.7 5.0 copy-start.35
  241.7 18.0 %slice-start = ((s8[4718592]{0:T(1024)(128)(4,1)}), s8[524288]{0:T(1024)(128)(4,1)S(1)}, s32[]{:S(2)}) async-start(s8[4718592]{0:T(1024)(128)(4,1)} %bitcast.164), calls=%async_computation.3 | async-start | bytes 1048576
  247.5 7.6 %copy-start.14 = (bf16[2048,384]{0,1:T(8,128)(2,1)S(1)}, bf16[2048,384]{0,1:T(8,128)(2,1)}, u32[]{:S(2)}) copy-start(bf16[2048,384]{0,1:T(8,128)(2,1)} %get-tuple-element.95) | copy-start | bytes 4718596
  247.5 12.1 %slice-start.1 = ((s8[4718592]{0:T(1024)(128)(4,1)}), s8[4194304]{0:T(1024)(128)(4,1)S(1)}, s32[]{:S(2)}) async-start(s8[4718592]{0:T(1024)(128)(4,1)} %bitcast.164), calls=%async_computation.4 | async-start | bytes 8388608
  273.3 55.6 %copy-start.25 = (f32[2,192]{1,0:T(2,128)S(1)}, f32[2,192]{1,0:T(2,128)}, u32[]{:S(2)}) copy-start(f32[2,192]{1,0:T(2,128)} %copy-done.24) | copy-start | bytes 4612
  332.8 201.2 %all-to-all-start.1 = ((f32[8,1,2880]{2,1,0:T(1,128)}), f32[8,1,2880]{2,1,0:T(1,128)S(1)}, u32[]{:S(2)}, u32[]{:S(2)}) async-start(f32[8,1,2880]{2,1,0:T(1,128)} %copy.63), calls=%async_computation.1 | async-start | bytes 188416 | tf_op jit(solution)/shard_map/all_to_all | solution.py:860
  534.1 9.1 %collective-permute-start.11 = (f32[1152]{0:T(1024)S(1)}, f32[1152]{0:T(1024)S(1)}, u32[]{:S(2)}, u32[]{:S(2)}) collective-permute-start(f32[1152]{0:T(1024)S(1)} %slice_reduce_fusion), channel_id=1, source_target_pairs={{24,0},{0,8},{8,16},{16,24},{25,1},{1,9},{9,17},{17,25},{26,2},{2,... | collective-permute-start | bytes 13832 | tf_op jit(solution)/shard_map/ppermute | solution.py:681
  534.7 8.6 %collective-permute-start.10 = (f32[1152]{0:T(1024)S(1)}, f32[1152]{0:T(1024)S(1)}, u32[]{:S(2)}, u32[]{:S(2)}) collective-permute-start(f32[1152]{0:T(1024)S(1)} %slice_reduce_fusion), channel_id=1, source_target_pairs={{16,0},{24,8},{0,16},{8,24},{17,1},{25,9},{1,17},{9,25},{18,2},{26... | collective-permute-start | bytes 13832 | tf_op jit(solution)/shard_map/ppermute | solution.py:681
  535.7 8.8 %collective-permute-start.9 = (f32[1152]{0:T(1024)S(1)}, f32[1152]{0:T(1024)S(1)}, u32[]{:S(2)}, u32[]{:S(2)}) collective-permute-start(f32[1152]{0:T(1024)S(1)} %slice_reduce_fusion), channel_id=1, source_target_pairs={{8,0},{16,8},{24,16},{0,24},{9,1},{17,9},{25,17},{1,25},{10,2},{18... | collective-permute-start | bytes 13832 | tf_op jit(solution)/shard_map/ppermute | solution.py:681
  539.5 15.4 %all-to-all-start.2 = ((bf16[8,2,1152]{2,1,0:T(2,128)(2,1)}), bf16[8,2,1152]{2,1,0:T(2,128)(2,1)S(1)}, u32[]{:S(2)}, u32[]{:S(2)}) async-start(bf16[8,2,1152]{2,1,0:T(2,128)(2,1)} %reshape.408), calls=%async_computation.2 | async-start | bytes 73728 | tf_op jit(solution)/shard_map/all_to_all | solution.py:874
  543.3 7.6 %collective-permute-start = (bf16[16,1152]{1,0:T(8,128)(2,1)S(1)}, bf16[16,1152]{1,0:T(8,128)(2,1)S(1)}, u32[]{:S(2)}, u32[]{:S(2)}) collective-permute-start(bf16[16,1152]{1,0:T(8,128)(2,1)S(1)} %fusion.41), channel_id=1, source_target_pairs={{8,0},{16,8},{24,16},{0,24},{9,1},{17,9},{25,17},{1,25},{10,2},{18... | collective-permute-start | bytes 110600 | tf_op jit(solution)/shard_map/ppermute | solution.py:681
  543.3 5.1 collective-permute-start.4
  544.5 2.7 collective-permute-start.3
  547.2 3.6 collective-permute-start.5
  (29 other events, 87.8 us)

commit v2 on v1

--- a/solution.py
+++ b/solution.py
@@ -298,23 +298,24 @@
                 pltpu.VMEM((n, way.outers, rows[a], width), BF16),
                 pltpu.VMEM((n if way.use_outer else 1, rows[a], width), BF16),
                 pltpu.VMEM((2, way.steps + 1, rows[a], width), BF16),
-                pltpu.VMEM((way.shares, rows[a], width), BF16),
+                pltpu.VMEM((n, way.outers, rows[a], width), BF16),
                 pltpu.VMEM((1, rows[a], width), BF16),
             ]
         a = way.arrays
         shapes += sem_pair(2, a, way.steps + 2) + sem_pair(a, n) + sem_pair(2, a, n)
-        return shapes + sem_pair(a) + sem_pair(2, a)
+        return shapes + sem_pair(a) + sem_pair(2, a) + [pltpu.SemaphoreType.DMA((2, a, n))]
 
     @staticmethod
     def scratch_count(way):
-        return 5 * way.arrays + 10
-
-    def __init__(self, way, links, parts, scratch):
-        self.way, self.links, self.parts = way, links, parts
+        return 5 * way.arrays + 11
+
+    def __init__(self, way, links, parts, outs, scratch):
+        self.way, self.links, self.parts, self.total = way, links, parts, outs
         bufs, sems = scratch[: 5 * way.arrays], scratch[5 * way.arrays :]
-        self.acc, self.cross, self.land, self.total, self.other = (bufs[k::5] for k in range(5))
+        self.acc, self.cross, self.land, self.own, self.other = (bufs[k::5] for k in range(5))
         self.ring, self.outer, self.core = sems[0:2], sems[2:4], sems[4:6]
         self.last_outer, self.last_core = sems[6:8], sems[8:10]
+        self.fetched = sems[10]
         self.pending = []
 
     def part(self, a, index, **flips):
@@ -328,6 +329,21 @@
 
     def order(self):
         return list(range(len(self.way.distances)))[::-1]
+
+    def fetch(self, a, index, o):
+        return pltpu.make_async_copy(
+            self.part(a, index, outer_flip=o), self.own[a].at[index, o], self.fetched.at[o, a, index]
+        )
+
+    def fetch_all(self):
+        for index in self.order():
+            for o in range(self.way.outers)[::-1]:
+                for a in range(self.way.arrays):
+                    self.fetch(a, index, o).start()
+
+    def fetched_part(self, a, index, o):
+        self.fetch(a, index, o).wait()
+        return self.own[a].at[index, o]
 
     def swap(self, index):
         way = self.way
@@ -350,14 +366,14 @@
             for a in range(way.arrays):
                 self.wait_swap(a, index, 1)
                 slot = self.acc[a].at[index, 1]
-                terms = [self.part(a, index, outer_flip=1)] + ([slot] if way.use_core else [])
+                terms = [self.fetched_part(a, index, 1)] + ([slot] if way.use_core else [])
                 sum_rows(slot, terms)
                 self.send(slot, self.cross[a].at[index], self.outer, (a, index), self.links.across())
 
     def terms(self, a, index):
         way = self.way
         self.wait_swap(a, index, 0)
-        terms = [self.part(a, index)] + ([self.acc[a].at[index, 0]] if way.use_core else [])
+        terms = [self.fetched_part(a, index, 0)] + ([self.acc[a].at[index, 0]] if way.use_core else [])
         if way.use_outer:
             slot = self.cross[a].at[index]
             remote(slot, slot, self.outer, (a, index), self.links.across()).wait_recv()
@@ -450,16 +466,13 @@
                 sum_rows(slot, [self.acc[a].at[0, 0], other])
                 self.send(slot, slot, self.last_core, (0, a), self.links.sibling())
 
-    def finish(self, outs):
+    def finish(self):
         way = self.way
         if way.use_core:
             for a in range(way.arrays):
                 for o in range(way.outers):
                     slot = self.total[a].at[way.share(self.links, outer_flip=o, core_flip=1)]
                     remote(slot, slot, self.last_core, (o, a), self.links.sibling()).wait_recv()
-        for a in range(way.arrays):
-            for share in range(way.shares):
-                sum_rows(outs[a].at[share], [self.total[a].at[share]])
         for copy in self.pending:
             copy.wait_send()
 
@@ -468,31 +481,48 @@
     links = Links(tp_count, grp_count)
     arrays = sum(way.arrays for way in ways)
     parts, outs, scratch = refs[:arrays], refs[arrays : 2 * arrays], refs[2 * arrays :]
-    reduces, at, low = [], 0, 0
+    only, at, low = [], 0, 0
     for way in ways:
         count = Reduce.scratch_count(way)
-        reduces.append((Reduce(way, links, parts[at : at + way.arrays], scratch[low : low + count]), outs[at : at + way.arrays]))
+        span = slice(at, at + way.arrays)
+        only.append(Reduce(way, links, parts[span], outs[span], scratch[low : low + count]))
         at += way.arrays
         low += count
+    for reduce in only:
+        reduce.fetch_all()
     links.greet(any(w.use_core for w in ways), True, any(w.use_core for w in ways))
-    only = [r for r, _ in reduces]
-    for index in only[0].order():
-        for reduce in only:
-            reduce.swap(index)
-    for index in only[0].order():
-        for reduce in only:
-            reduce.crossing(index)
-    for reduce in only:
-        reduce.opposite()
-    for step in range(only[0].way.steps, 0, -1):
-        for reduce in only:
-            reduce.step(step)
-    for reduce in only:
-        reduce.close()
-    for reduce in only:
-        reduce.share_out()
-    for reduce, out in reduces:
-        reduce.finish(out)
+    for stage in reduce_stages(only):
+        stage()
+
+
+def reduce_stages(reduces):
+    way = reduces[0].way
+    order, steps = reduces[0].order(), way.steps
+
+    def swaps():
+        for index in order:
+            for reduce in reduces:
+                reduce.swap(index)
+
+    def every(name, *args):
+        def stage():
+            for reduce in reduces:
+                getattr(reduce, name)(*args)
+
+        return stage
+
+    stages = [swaps]
+    if len(way.distances) % 2 == 0:
+        stages.append(every("crossing", order[0]))
+    for side in (2 * steps, 2 * steps - 1):
+        stages.append(every("crossing", side))
+    stages.append(every("opposite"))
+    for step in range(steps, 0, -1):
+        ahead = [2 * step - 2, 2 * step - 3] if step > 1 else [0]
+        for index in ahead:
+            stages.append(every("crossing", index))
+        stages.append(every("step", step))
+    return stages + [every("close"), every("share_out"), every("finish")]
 
 
 def reduce_weights(ways, parts, tp_count, grp_count, collective_id):
@@ -505,9 +535,9 @@
     vmem = pl.BlockSpec(memory_space=pltpu.VMEM)
     return pl.pallas_call(
         functools.partial(reduce_kernel, ways, tp_count, grp_count),
-        in_specs=[vmem] * len(parts),
+        in_specs=[pl.BlockSpec(memory_space=pltpu.HBM)] * len(parts),
         out_specs=[vmem] * len(parts),
-        out_shape=[jax.ShapeDtypeStruct(x.shape[1:], F32) for x in parts],
+        out_shape=[jax.ShapeDtypeStruct(x.shape[1:], BF16) for x in parts],
         scratch_shapes=scratch,
         compiler_params=pltpu.CompilerParams(collective_id=collective_id, has_side_effects=True),
     )(*parts)

time: 567 us -> 551 us (0.972)
  Pallas kernels: 386 us -> 371 us
    pallas_call x2, Pallas kernels: 182 us -> 167 us  [reduce_weights(): pl.pallas_call(functools.partial(reduce_kernel, ways, tp_count, grp_count...]
  transfers between devices with their start and end apart: 15 -> 15, of which waited for: 1 -> 1; matrix products, arithmetic and copies ran while one was open for 24% -> 25% of each run, Pallas kernels for 69% -> 69%
where the time goes in v2:
time: 551 us; the launch traced here: 541 us
  Pallas kernels  371 us (67%)
  matrix products  76 us (14%)
  other arithmetic  35.7 us (6%)
  local copies, waits for them, and re-layouts  28.2 us (5%)
  starting transfers between devices  24.7 us (4%)
    pallas_call x2, Pallas kernels, reduce_weights(): pl.pallas_call(functools.partial(reduce_kernel, ways, tp_count, grp_count...  167 us
    pallas_call x1, Pallas kernels, gather_weights(): pl.pallas_call(functools.partial(gather_kernel, ways, set_sizes, tp_count...  123 us
    dot_general x12, matrix products, dot(): return lax.dot_general(a, b, dims, preferred_element_type=F32)  60.1 us
    pallas_call x1, Pallas kernels, attend_back(): pl.pallas_call(functools.partial(attend_back_kernel, images), grid=(shard...  50 us
    pallas_call x1, Pallas kernels, attend(): pl.pallas_call(functools.partial(attend_kernel, images), grid=(shards * l...  30.9 us
  transfers between devices with their start and end apart: 15, of which 1 were waited for; matrix products, arithmetic and copies ran while one was open for 25% of the time, Pallas kernels for 69%

profile of v2, /device:TPU:0, one launch (start us, length us, event | category | flops | bytes accessed | tf_op | source)
XLA Modules:
  0.0 540.9 jit_solution(8127116639206887895)
XLA Ops:
  0.7 2.5 collective-permute-start.6
  10.5 5.8 %all-to-all-start = ((f32[8,1,2592]{2,1,0:T(1,128)}), f32[8,1,2592]{2,1,0:T(1,128)S(1)}, u32[]{:S(2)}, u32[]{:S(2)}) async-start(f32[8,1,2592]{2,1,0:T(1,128)} %copy.57), calls=%async_computation | async-start | bytes 172032 | tf_op jit(solution)/shard_map/all_to_all | solution.py:788
  18.9 2.0 slice.104
  23.4 2.0 copy.59
  32.8 123.5 %shard_map.254 = (bf16[8,4,72,1152]{3,2,1,0:T(8,128)(2,1)}, bf16[8,2,144,1152]{3,2,1,0:T(8,128)(2,1)}, bf16[8,4,80,1152]{3,2,1,0:T(8,128)(2,1)}, bf16[8,2,128,11...) custom-call(bf16[72,1152]{1,0:T(8,128)(2,1)} %dynamic-slice_bitcast_fusion.5.refs_0_, ...), custom_call_target="tpu_custom_call" | custom-call | tf_op jit(solution)/shard_map/pallas_call | solution.py:258
  162.0 2.8 add_convert_fusion.5
  164.8 30.9 %shard_map.255 = (bf16[8,2,384,144]{3,2,1,0:T(8,128)(2,1)}, bf16[8,2,384,72]{3,2,1,0:T(8,128)(2,1)}, bf16[8,2,384,72]{3,2,1,0:T(8,128)(2,1)}, f32[384,1152]{1,0:T(8,128)}) custom-call(bf16[384,1152]{1,0:T(8,128)(2,1)} %bitcast.155, bf16[8,2,144,1152]{3,2,1,0:T(8,128)(2,1)} %get-tuple-element.35.qk_ref.qkw_ref, bf16[8,2,2,72,1152]{4,3,2,1,0:T(8,128)(2,1)} %bitcast.146, ...), custom_call_target="tpu_custom_call" | custom-call | tf_op jit(solution)/shard_map/pallas_call | solution.py:590
  195.7 2.4 fusion.52
  202.1 5.4 convolution_add_fusion
  207.5 4.7 fusion.51
  212.2 4.8 convert_reduce_fusion
  217.0 5.6 %convolution_convert_fusion.1 = bf16[2560,1152]{1,0:T(8,128)(2,1)} fusion(bf16[384,1152]{1,0:T(8,128)(2,1)S(1)} %bitcast.185, f32[2560,384]{0,1:T(8,128)S(1)} %convolution_add_fusion), kind=kOutput, calls=%fused_computation.1 | convolution fusion | flops 2276720640 | bytes 10715136 | tf_op jit(solution)/shard_map/dot_general | solution.py:20
  222.7 3.9 fusion.57
  226.6 5.3 convolution_convert_fusion
  232.0 4.7 fusion.56
  236.7 4.9 convolution_convert_fusion.3
  241.7 5.2 convert_reduce_fusion.1
  247.5 7.6 %convolution_add_fusion.4 = f32[384,1152]{1,0:T(8,128)} fusion(f32[384,1152]{1,0:T(8,128)} %fusion.51, bf16[2048,1152]{1,0:T(8,128)(2,1)} %bitcast.218, f32[2048,384]{0,1:T(8,128)} %copy-done.32, f32[2048]{0:T(1024)S(1)} %bitcast.209), kind=kOutput, calls=%fused_computation.20 | convolution fusion | flops 1820246016 | bytes 11411456 | tf_op jit(solution)/shard_map/dot_general | solution.py:20
  255.1 4.5 convolution_convert_fusion.2
  259.6 3.4 fusion.3
  263.2 2.8 multiply_reduce_fusion.1
  266.3 3.8 convolution_add_fusion.2
  273.2 50.0 %shard_map.256 = (bf16[8,2,144,1152]{3,2,1,0:T(8,128)(2,1)}, bf16[8,2,2,72,1152]{4,3,2,1,0:T(8,128)(2,1)}, f32[8,2,1,144]{3,2,1,0:T(1,128)}, f32[8,2,1,72]{3,2,1,0:T(1,128)}, f32[384,1152]{1,0:T(8,128)}) custom-call(bf16[384,1152]{1,0:T(8,128)(2,1)} %bitcast.156, bf16[384,1152]{1,0:T(8,128)(2,1)} %bitcast.168, ...), custom_call_target="tpu_custom_call" | custom-call | tf_op jit(solution)/shard_map/pallas_call | solution.py:656
  328.2 2.7 multiply_reduce_fusion.3
  332.2 4.5 all-to-all-start.1
  336.7 64.3 %shard_map.257 = (bf16[4,72,1152]{2,1,0:T(8,128)(2,1)}, bf16[2,144,1152]{2,1,0:T(8,128)(2,1)}) custom-call(bf16[8,4,72,1152]{3,2,1,0:T(8,128)(2,1)} %bitcast.161, bf16[8,2,144,1152]{3,2,1,0:T(8,128)(2,1)} %get-tuple-element.49.refs_1_), custom_call_target="tpu_custom_call" | custom-call | tf_op jit(solution)/shard_map/pallas_call | solution.py:536
  405.2 4.5 convolution_add_fusion.1
  409.7 102.3 %shard_map.258 = (bf16[4,80,1152]{2,1,0:T(8,128)(2,1)}, bf16[2,128,1152]{2,1,0:T(8,128)(2,1)}, bf16[4,80,1152]{2,1,0:T(8,128)(2,1)}, bf16[2,128,1152]{2,1,0:T(8,128)(2,1)}) custom-call(bf16[8,4,80,1152]{3,2,1,0:T(8,128)(2,1)} %bitcast.159, bf16[8,2,128,1152]{3,2,1,0:T(8,128)(2,1)} %bitcast.166, bf16[8,4,80,1152]{3,2,1,0:T(8,128)(2,1)} %bitcast.160, ...), custom_call_target="tpu_custom_call" | custom-call | tf_op jit(solution)/shard_map/pallas_call | solution.py:536
  512.0 3.1 divide_bitcast_fusion
  523.8 3.7 all-to-all-start.2
  532.5 2.4 collective-permute-done.5
  535.0 3.5 convolution_divide_fusion
  (229 shorter events, 58.5 us)
Async XLA Ops:
  0.6 7.3 %copy-start = (bf16[1152,6,144]{0,2,1:T(8,128)(2,1)S(1)}, bf16[1152,6,144]{0,2,1:T(8,128)(2,1)}, u32[]{:S(2)}) copy-start(bf16[1152,6,144]{0,2,1:T(8,128)(2,1)} %param.19) | copy-start | bytes 5971972
  0.7 15.7 %copy-start.31 = (s32[16]{0:T(128)S(1)}, s32[16]{0:T(128)}, u32[]{:S(2)}) copy-start(s32[16]{0:T(128)} %param.17) | copy-start | bytes 196
  0.7 8.9 %copy-start.30 = (bf16[576]{0:T(1024)(128)(2,1)S(1)}, bf16[576]{0:T(1024)(128)(2,1)}, u32[]{:S(2)}) copy-start(bf16[576]{0:T(1024)(128)(2,1)} %param.26) | copy-start | bytes 3460
  0.7 155.7 %collective-permute-start.6 = (s32[16]{0:T(128)}, s32[16]{0:T(128)}, u32[]{:S(2)}, u32[]{:S(2)}) collective-permute-start(s32[16]{0:T(128)} %param.17), channel_id=1, source_target_pairs={{8,0},{16,8},{24,16},{0,24},{9,1},{17,9},{25,17},{1,25},{10,2},{18... | collective-permute-start | bytes 200 | tf_op jit(solution)/shard_map/ppermute | solution.py:711
  3.2 153.2 %collective-permute-start.8 = (s32[16]{0:T(128)}, s32[16]{0:T(128)}, u32[]{:S(2)}, u32[]{:S(2)}) collective-permute-start(s32[16]{0:T(128)} %param.17), channel_id=1, source_target_pairs={{24,0},{0,8},{8,16},{16,24},{25,1},{1,9},{9,17},{17,25},{26,2},{2,... | collective-permute-start | bytes 200 | tf_op jit(solution)/shard_map/ppermute | solution.py:711
  3.2 153.2 %collective-permute-start.7 = (s32[16]{0:T(128)}, s32[16]{0:T(128)}, u32[]{:S(2)}, u32[]{:S(2)}) collective-permute-start(s32[16]{0:T(128)} %param.17), channel_id=1, source_target_pairs={{16,0},{24,8},{0,16},{8,24},{17,1},{25,9},{1,17},{9,25},{18,2},{26... | collective-permute-start | bytes 200 | tf_op jit(solution)/shard_map/ppermute | solution.py:711
  5.0 530.0 %collective-permute-start.2 = (bf16[16,1152]{1,0:T(8,128)(2,1)S(1)}, bf16[16,1152]{1,0:T(8,128)(2,1)}, u32[]{:S(2)}, u32[]{:S(2)}) collective-permute-start(bf16[16,1152]{1,0:T(8,128)(2,1)S(1)} %fusion.39), channel_id=1, source_target_pairs={{24,0},{0,8},{8,16},{16,24},{25,1},{1,9},{9,17},{17,25},{26,2},{2,... | collective-permute-start | bytes 110600 | tf_op jit(solution)/shard_map/ppermute | solution.py:711
  5.9 529.1 %collective-permute-start.1 = (bf16[16,1152]{1,0:T(8,128)(2,1)S(1)}, bf16[16,1152]{1,0:T(8,128)(2,1)}, u32[]{:S(2)}, u32[]{:S(2)}) collective-permute-start(bf16[16,1152]{1,0:T(8,128)(2,1)S(1)} %fusion.39), channel_id=1, source_target_pairs={{16,0},{24,8},{0,16},{8,24},{17,1},{25,9},{1,17},{9,25},{18,2},{26... | collective-permute-start | bytes 110600 | tf_op jit(solution)/shard_map/ppermute | solution.py:711
  9.4 11.4 %copy-start.16 = (bf16[1152,576]{0,1:T(8,128)(2,1)S(1)}, bf16[1152,576]{0,1:T(8,128)(2,1)}, u32[]{:S(2)}) copy-start(bf16[1152,576]{0,1:T(8,128)(2,1)} %param.25) | copy-start | bytes 3981316
  10.5 149.7 %all-to-all-start = ((f32[8,1,2592]{2,1,0:T(1,128)}), f32[8,1,2592]{2,1,0:T(1,128)S(1)}, u32[]{:S(2)}, u32[]{:S(2)}) async-start(f32[8,1,2592]{2,1,0:T(1,128)} %copy.57), calls=%async_computation | async-start | bytes 172032 | tf_op jit(solution)/shard_map/all_to_all | solution.py:788
  17.1 181.4 %copy-start.25 = (pred[2,192]{1,0:T(4,128)(4,1)}, pred[2,192]{1,0:T(4,128)(4,1)S(1)}, u32[]{:S(2)}) copy-start(pred[2,192]{1,0:T(4,128)(4,1)S(1)} %get-tuple-element.84) | copy-start | bytes 1156
  27.5 134.5 %copy-start.23 = (f32[2,192]{1,0:T(2,128)}, f32[2,192]{1,0:T(2,128)S(1)}, u32[]{:S(2)}) copy-start(f32[2,192]{1,0:T(2,128)S(1)} %add_rsqrt_fusion.1) | copy-start | bytes 4612
  201.7 15.3 %copy-start.18 = (bf16[2,192,1152]{2,1,0:T(8,128)(2,1)}, bf16[2,192,1152]{2,1,0:T(8,128)(2,1)S(1)}, u32[]{:S(2)}) copy-start(bf16[2,192,1152]{2,1,0:T(8,128)(2,1)S(1)} %get-tuple-element.67) | copy-start | bytes 2654212
  201.7 5.8 %slice-start.6 = ((s8[5898240]{0:T(1024)(128)(4,1)}), s8[4194304]{0:T(1024)(128)(4,1)S(1)}, s32[]{:S(2)}) async-start(s8[5898240]{0:T(1024)(128)(4,1)} %bitcast.214), calls=%async_computation.9 | async-start | bytes 8388608
  202.1 5.4 slice-start.7
  207.5 15.1 %slice-start.4 = ((s8[5898240]{0:T(1024)(128)(4,1)}), s8[4194304]{0:T(1024)(128)(4,1)S(1)}, s32[]{:S(2)}) async-start(s8[5898240]{0:T(1024)(128)(4,1)} %bitcast.211), calls=%async_computation.7 | async-start | bytes 8388608
  212.2 10.5 %slice-start.5 = ((s8[5898240]{0:T(1024)(128)(4,1)}), s8[1703936]{0:T(1024)(128)(4,1)S(1)}, s32[]{:S(2)}) async-start(s8[5898240]{0:T(1024)(128)(4,1)} %bitcast.211), calls=%async_computation.8 | async-start | bytes 3407872
  231.9 9.7 %slice-start.8 = ((s8[4718592]{0:T(1024)(128)(4,1)}), s8[4194304]{0:T(1024)(128)(4,1)S(1)}, s32[]{:S(2)}) async-start(s8[4718592]{0:T(1024)(128)(4,1)} %bitcast.219), calls=%async_computation.11 | async-start | bytes 8388608
  236.7 5.0 copy-start.32
  241.6 18.0 %slice-start = ((s8[4718592]{0:T(1024)(128)(4,1)}), s8[524288]{0:T(1024)(128)(4,1)S(1)}, s32[]{:S(2)}) async-start(s8[4718592]{0:T(1024)(128)(4,1)} %bitcast.163), calls=%async_computation.3 | async-start | bytes 1048576
  247.5 7.6 %copy-start.14 = (bf16[2048,384]{0,1:T(8,128)(2,1)S(1)}, bf16[2048,384]{0,1:T(8,128)(2,1)}, u32[]{:S(2)}) copy-start(bf16[2048,384]{0,1:T(8,128)(2,1)} %get-tuple-element.93) | copy-start | bytes 4718596
  247.5 12.1 %slice-start.1 = ((s8[4718592]{0:T(1024)(128)(4,1)}), s8[4194304]{0:T(1024)(128)(4,1)S(1)}, s32[]{:S(2)}) async-start(s8[4718592]{0:T(1024)(128)(4,1)} %bitcast.163), calls=%async_computation.4 | async-start | bytes 8388608
  273.2 55.0 %copy-start.24 = (f32[2,192]{1,0:T(2,128)S(1)}, f32[2,192]{1,0:T(2,128)}, u32[]{:S(2)}) copy-start(f32[2,192]{1,0:T(2,128)} %copy-done.23) | copy-start | bytes 4612
  332.2 186.0 %all-to-all-start.1 = ((f32[8,1,2880]{2,1,0:T(1,128)}), f32[8,1,2880]{2,1,0:T(1,128)S(1)}, u32[]{:S(2)}, u32[]{:S(2)}) async-start(f32[8,1,2880]{2,1,0:T(1,128)} %copy.63), calls=%async_computation.1 | async-start | bytes 188416 | tf_op jit(solution)/shard_map/all_to_all | solution.py:890
  518.3 9.1 %collective-permute-start.11 = (f32[1152]{0:T(1024)S(1)}, f32[1152]{0:T(1024)S(1)}, u32[]{:S(2)}, u32[]{:S(2)}) collective-permute-start(f32[1152]{0:T(1024)S(1)} %slice_reduce_fusion), channel_id=1, source_target_pairs={{24,0},{0,8},{8,16},{16,24},{25,1},{1,9},{9,17},{17,25},{26,2},{2,... | collective-permute-start | bytes 13832 | tf_op jit(solution)/shard_map/ppermute | solution.py:711
  518.8 8.7 %collective-permute-start.10 = (f32[1152]{0:T(1024)S(1)}, f32[1152]{0:T(1024)S(1)}, u32[]{:S(2)}, u32[]{:S(2)}) collective-permute-start(f32[1152]{0:T(1024)S(1)} %slice_reduce_fusion), channel_id=1, source_target_pairs={{16,0},{24,8},{0,16},{8,24},{17,1},{25,9},{1,17},{9,25},{18,2},{26... | collective-permute-start | bytes 13832 | tf_op jit(solution)/shard_map/ppermute | solution.py:711
  519.8 8.7 %collective-permute-start.9 = (f32[1152]{0:T(1024)S(1)}, f32[1152]{0:T(1024)S(1)}, u32[]{:S(2)}, u32[]{:S(2)}) collective-permute-start(f32[1152]{0:T(1024)S(1)} %slice_reduce_fusion), channel_id=1, source_target_pairs={{8,0},{16,8},{24,16},{0,24},{9,1},{17,9},{25,17},{1,25},{10,2},{18... | collective-permute-start | bytes 13832 | tf_op jit(solution)/shard_map/ppermute | solution.py:711
  523.8 15.3 %all-to-all-start.2 = ((bf16[8,2,1152]{2,1,0:T(2,128)(2,1)}), bf16[8,2,1152]{2,1,0:T(2,128)(2,1)S(1)}, u32[]{:S(2)}, u32[]{:S(2)}) async-start(bf16[8,2,1152]{2,1,0:T(2,128)(2,1)} %reshape.409), calls=%async_computation.2 | async-start | bytes 73728 | tf_op jit(solution)/shard_map/all_to_all | solution.py:904
  527.4 7.6 %collective-permute-start = (bf16[16,1152]{1,0:T(8,128)(2,1)S(1)}, bf16[16,1152]{1,0:T(8,128)(2,1)S(1)}, u32[]{:S(2)}, u32[]{:S(2)}) collective-permute-start(bf16[16,1152]{1,0:T(8,128)(2,1)S(1)} %fusion.39), channel_id=1, source_target_pairs={{8,0},{16,8},{24,16},{0,24},{9,1},{17,9},{25,17},{1,25},{10,2},{18... | collective-permute-start | bytes 110600 | tf_op jit(solution)/shard_map/ppermute | solution.py:711
  527.5 5.0 collective-permute-start.4
  528.5 2.8 collective-permute-start.3
  531.3 3.6 collective-permute-start.5
  (26 other events, 82.9 us)
